TPU v7x, 128 devices: a whole 4x4x4 slice. The times are simulated.
128 devices in a mesh: tile: 8 (over z, core), focus: 16 (over x, y).
Axes of the slice: x: 4, y: 4, z: 4, core: 2. Of those that a mesh axis runs over, the one named last changes fastest.
Arguments:
- mask_tiles: bfloat16 [1024, 512, 512], P(('tile', 'focus')), may hold values from -1 to 1
- class_of_tile: int32 [1024, 1], P(('tile', 'focus')), may hold values from 0 to 15; in each aligned block of 8 rows (0 to 7, 8 to 15, ...) at most 2 rows name the same one
- cell_of_tile: int32 [1024], P(('tile', 'focus')), may hold values from 0 to 1023
- kernels: bfloat16 [16, 24, 4, 4096], P('focus'), may hold values from -0.19921875 to 0.19921875
- class_center: float32 [16], replicated, may hold values from -0.6 to 0.6
Outputs:
- resist_image: bfloat16 [1024, 512, 512], P(('tile', 'focus'))
Inputs may be any that keep to these rules, and one draw needn't show every extreme that they name: `class_of_tile`: the 8 tiles of one device hold at most 2 tiles of any one class.
All inputs are finite; a program needn't handle non-finite values.
Results may differ from a plain program's by a relative error of at most 0.009.
Values may be sent and summed in bfloat16 or wider, within the bound.
No kernel may reach another device: no remote copies, remote signals or barrier semaphores. Data moves between devices by JAX's collectives and lax.ppermute only.
A program may use at most 128 MiB of HBM per device.

v0:
```python
import functools

import jax
import jax.numpy as jnp
import numpy as np
from jax import lax
from jax.experimental import pallas as pl
from jax.experimental.pallas import tpu as pltpu
from jax.sharding import PartitionSpec as P


P_SIZE = 512
NF = 64
KER = 24
BLK_PX = 64
SC = 32
Q = 128
B = 8
REACH = 64
GRID = SC * B
HALF = KER // 2
GROUPS = HALF // 4
TILES = 8
GAIN_SCALE = 50.0
ALL = ("tile", "focus")
BEST = lax.Precision.HIGHEST
F32 = jnp.float32
BF16 = jnp.bfloat16


def spectral_table(freq_count, length):
    frequency = np.arange(freq_count) - freq_count // 2
    phases = np.mod(frequency[:, None] * np.arange(length)[None, :], length) * (2.0 * np.pi / length)
    return np.cos(phases), np.sin(phases)


def wave_table():
    return np.concatenate(spectral_table(NF, P_SIZE), axis=0)


def left_table():
    c, s = spectral_table(NF, Q)
    return np.concatenate(
        [np.concatenate([c.T, -s.T], axis=1), np.concatenate([s.T, c.T], axis=1)], axis=0
    )


def pair_table():
    c, s = spectral_table(NF, Q)
    z = np.zeros((NF, 2 * Q))
    up = np.concatenate([c, s], axis=1)
    down = np.concatenate([-s, c], axis=1)
    return np.block([[up, z], [z, up], [down, z], [z, down]])


def resist_table(pixels, samples):
    cos_pix, sin_pix = spectral_table(samples, pixels)
    cos_smp, sin_smp = spectral_table(samples, samples)
    frequency = np.arange(samples) - samples // 2
    weight = np.exp(-0.5 * (frequency * (4.0 / samples)) ** 2)[:, None]
    return ((cos_pix * weight).T @ cos_smp + (sin_pix * weight).T @ sin_smp) / samples


def spread_table(extent, length):
    places = np.arange(extent)
    weight = np.exp(-np.abs(places[:, None] - places[None, :]) / length)
    return weight / np.sum(weight, axis=1, keepdims=True)


def height_tables():
    spread = spread_table(GRID, REACH)
    rows = spread.reshape(SC, B, SC, B).mean(axis=1)
    cols = spread.reshape(SC, B, SC, B).mean(axis=3)
    row_part = np.tile(rows.transpose(1, 2, 0), (1, 1, 4))
    col_part = np.tile(cols, (1, 1, 4)) / (BLK_PX * BLK_PX)
    return row_part.astype(np.float32), col_part.astype(np.float32)


def as_bf16(table):
    return jnp.asarray(table.astype(np.float32)).astype(BF16)


def fixed(*shape):
    return pl.BlockSpec(shape, lambda *_: (0,) * len(shape))


def tiles(count, *shape):
    return pl.BlockSpec((count, *shape), lambda t: (t,) + (0,) * len(shape))


SMEM = pl.BlockSpec(memory_space=pltpu.SMEM)
VMEM = pl.BlockSpec(memory_space=pltpu.VMEM)
ANY = pl.BlockSpec(memory_space=pl.ANY)


def analyse_kernel(cell_ref, mask_hbm, wave_t_ref, wave_ref, row_ref, col_ref, spec_ref, height_ref, mask, rows, along, sems):
    def copy(t):
        return pltpu.make_async_copy(mask_hbm.at[t], mask.at[t], sems.at[t])

    for t in range(TILES):
        copy(t).start()
    lower = lax.broadcasted_iota(jnp.int32, (NF, 2 * NF), 1) < NF
    left = lax.broadcasted_iota(jnp.int32, (B, 2 * BLK_PX), 1) < BLK_PX
    scale = 1.0 / P_SIZE

    def some_tiles(trip, carry):
        batch = [trip * 2, trip * 2 + 1]
        for t in batch:
            copy(t).wait()
        for t in batch:
            cell = cell_ref[t]
            at = pl.ds(pl.multiple_of(t * B, B), B)
            col = col_ref[cell & (SC - 1)]
            wide = mask[t].astype(F32)
            sums = jnp.sum((wide * wide).reshape(B, BLK_PX, P_SIZE), axis=1)
            spread = jnp.zeros((B, 4 * SC), F32)
            for pair in range(B // 2):
                two = sums[:, pair * 2 * BLK_PX : (pair + 1) * 2 * BLK_PX]
                first = jnp.sum(jnp.where(left, two, 0.0), axis=1, keepdims=True)
                second = jnp.sum(jnp.where(left, 0.0, two), axis=1, keepdims=True)
                spread = spread + first * col[2 * pair : 2 * pair + 1] + second * col[2 * pair + 1 : 2 * pair + 2]
            along[at, :] = spread
            rows[at, :] = row_ref[cell // SC]
        for t in batch:
            projected = jnp.dot(mask[t], wave_t_ref[...], preferred_element_type=F32).astype(BF16)
            raw = jnp.dot(wave_ref[...], projected, preferred_element_type=F32)
            turned = pltpu.roll(raw, NF, 1)
            re = (raw[:NF] - turned[NF:]) * scale
            im = (turned[:NF] + raw[NF:]) * (-scale)
            spec_ref[t, 0] = jnp.where(lower, re, pltpu.roll(re, NF, 1)).astype(BF16)
            spec_ref[t, 1] = jnp.where(lower, im, pltpu.roll(im, NF, 1)).astype(BF16)
        return carry

    lax.fori_loop(0, TILES // 2, some_tiles, 0)
    whole = lax.dot_general(
        rows[...], along[...], (((0,), (0,)), ((), ())), precision=BEST, preferred_element_type=F32
    )
    quarter = lax.broadcasted_iota(jnp.int32, (B, 4 * SC), 1) // SC
    part = jnp.zeros((B, 4 * SC), F32)
    for q in range(4):
        part = jnp.where(quarter == q, whole[q * B : (q + 1) * B], part)
    height_ref[...] = part


def analyse(mask_tiles, cell_of_tile):
    wave = wave_table()
    row_part, col_part = height_tables()
    return pl.pallas_call(
        analyse_kernel,
        in_specs=[SMEM, ANY] + [VMEM] * 4,
        out_specs=[VMEM, VMEM],
        out_shape=[
            jax.ShapeDtypeStruct((TILES, 2, NF, 2 * NF), BF16),
            jax.ShapeDtypeStruct((B, 4 * SC), F32),
        ],
        scratch_shapes=[
            pltpu.VMEM((TILES, P_SIZE, P_SIZE), BF16),
            pltpu.VMEM((TILES * B, 4 * SC), F32),
            pltpu.VMEM((TILES * B, 4 * SC), F32),
            pltpu.SemaphoreType.DMA((TILES,)),
        ],
        name="analyse",
        cost_estimate=pl.CostEstimate(flops=10**9, bytes_accessed=6 * 10**6, transcendentals=0),
    )(cell_of_tile, mask_tiles, as_bf16(wave.T), as_bf16(wave), jnp.asarray(row_part), jnp.asarray(col_part))


def image_kernel(
    place_ref, class_ref, cell_ref, centre_ref, height_ref, spec_ref, left_ref, pair_ref, *rest
):
    pieces, (out_ref, held, sems) = rest[:8], rest[8:]

    def fetch(tile, carry):
        set_id = class_ref[tile]
        first = (place_ref[0] - (set_id // place_ref[2])) & 3
        second = (place_ref[1] - (set_id // place_ref[3])) & 3
        which = second * 2 + first // 2
        for at, ref in enumerate(pieces):

            @pl.when(which == at)
            def _():
                pltpu.make_async_copy(ref.at[first & 1], held.at[tile], sems.at[tile]).start()

        return carry

    lax.fori_loop(0, TILES, fetch, 0)
    heights = height_ref[...]
    mean = jnp.sum(heights, keepdims=True) * (1.0 / (SC * SC))
    height_row = lax.broadcasted_iota(jnp.int32, heights.shape, 0)
    height_lane = lax.broadcasted_iota(jnp.int32, heights.shape, 1)

    def some_tiles(trip, carry):
        batch = [trip * 2, trip * 2 + 1]
        for t in batch:
            pltpu.make_async_copy(pieces[0].at[0], held.at[t], sems.at[t]).wait()
        for t in batch:
            cell = cell_ref[t]
            row = cell // SC
            here = (height_row == (row & 7)) & (height_lane == (row // 8) * SC + (cell & (SC - 1)))
            shift = jnp.sum(jnp.where(here, heights, 0.0), keepdims=True) - mean
            shift = GAIN_SCALE * shift - centre_ref[class_ref[t]]
            re_part = spec_ref[t, 0].astype(F32)
            im_part = spec_ref[t, 1].astype(F32)
            re_part = jnp.concatenate([re_part, re_part], axis=1)
            im_part = jnp.concatenate([im_part, im_part], axis=1)
            filtered = []
            for g in range(GROUPS):
                kern_re = held[t, g, 0].astype(F32) + shift * held[t, g, 2].astype(F32)
                kern_im = held[t, g, 1].astype(F32) + shift * held[t, g, 3].astype(F32)
                prod_re = kern_re * re_part - kern_im * im_part
                prod_im = kern_re * im_part + kern_im * re_part
                filtered.append(jnp.concatenate([prod_re.astype(BF16), prod_im.astype(BF16)], axis=0))
            along = jnp.dot(
                left_ref[...], jnp.concatenate(filtered, axis=1), preferred_element_type=F32
            ).astype(BF16)
            both = [
                jnp.concatenate([along[:Q, at : at + 2 * NF], along[Q:, at : at + 2 * NF]], axis=1)
                for at in range(0, GROUPS * 4 * NF, 2 * NF)
            ]
            fields = jnp.dot(jnp.concatenate(both, axis=0), pair_ref[...], preferred_element_type=F32)
            total = jnp.zeros((Q, Q), F32)
            for part in range(4):
                for at in range(0, GROUPS * 2 * Q, Q):
                    block = fields[at : at + Q, part * Q : (part + 1) * Q]
                    total = total + block * block
            out_ref[t] = total.astype(out_ref.dtype)
        return carry

    lax.fori_loop(0, TILES // 2, some_tiles, 0)


def image(place, classes, cells, centre, heights, spectra, pieces, dtype):
    return pl.pallas_call(
        image_kernel,
        in_specs=[SMEM] * 4 + [VMEM] * 4 + [ANY] * 8,
        out_specs=VMEM,
        out_shape=jax.ShapeDtypeStruct((TILES, Q, Q), dtype),
        scratch_shapes=[
            pltpu.VMEM((TILES, GROUPS, 4, NF, 4 * NF), BF16),
            pltpu.SemaphoreType.DMA((TILES,)),
        ],
        name="image",
        cost_estimate=pl.CostEstimate(flops=3 * 10**9, bytes_accessed=4 * 10**6, transcendentals=0),
    )(place, classes, cells, centre, heights, spectra, as_bf16(left_table()), as_bf16(pair_table()), *pieces)


def resist_kernel(count, own_ref, other_ref, resist_ref, resist_t_ref, out_ref):
    intensity = (own_ref[...] + other_ref[...].astype(F32)) * (1.0 / KER)
    intensity = intensity.astype(BF16).reshape(count * Q, Q)
    half_way = jnp.dot(intensity, resist_t_ref[...], preferred_element_type=F32).astype(BF16)
    for t in range(count):
        out_ref[t] = jnp.dot(
            resist_ref[...], half_way[t * Q : (t + 1) * Q], preferred_element_type=F32
        ).astype(BF16)


def resist(own, other, count=4):
    table = resist_table(P_SIZE, Q)
    return pl.pallas_call(
        functools.partial(resist_kernel, count),
        grid=(TILES // count,),
        in_specs=[tiles(count, Q, Q), tiles(count, Q, Q), fixed(P_SIZE, Q), fixed(Q, P_SIZE)],
        out_specs=tiles(count, P_SIZE, P_SIZE),
        out_shape=jax.ShapeDtypeStruct((TILES, P_SIZE, P_SIZE), BF16),
        name="resist",
        cost_estimate=pl.CostEstimate(flops=10**9, bytes_accessed=5 * 10**6, transcendentals=0),
    )(own, other, as_bf16(table), as_bf16(table.T))


PLACES = [(z, core, x, y) for z in range(4) for core in range(2) for x in range(4) for y in range(4)]


def place_of(z, core, x, y):
    return ((z * 2 + core) * 4 + x % 4) * 4 + y % 4


def ring(phase, step):
    pairs = []
    for z, core, x, y in PLACES:
        along_y = (core + phase) % 2 == 0
        to = (z, core, x, y + step) if along_y else (z, core, x + step, y)
        pairs.append((place_of(z, core, x, y), place_of(*to)))
    return pairs


def send(value, phase, step):
    return lax.ppermute(value, ALL, ring(phase, step))


def after_all(value, *others):
    return lax.optimization_barrier((value, *others))[0]


def partner(x):
    return lax.ppermute(x, "tile", [(t, t ^ 1) for t in range(8)])


def summed(x, axis):
    size = lax.axis_size(axis)
    copies = jnp.broadcast_to(x[None], (size, *x.shape))
    return jnp.sum(lax.all_to_all(copies, axis, 0, 0, tiled=True), axis=0)


def device_steps(mask_tiles, class_of_tile, cell_of_tile, kernels, class_center):
    core = lax.axis_index("tile") % 2
    focus = lax.axis_index("focus")
    x, y = focus // 4, focus % 4
    place = jnp.stack(
        [
            jnp.where(core == 0, y, x),
            jnp.where(core == 0, x, y),
            jnp.where(core == 0, 1, 4),
            jnp.where(core == 0, 4, 1),
        ]
    ).astype(jnp.int32)
    classes = class_of_tile[:, 0]
    other_labels = partner(jnp.concatenate([classes, cell_of_tile]))

    mine = lax.dynamic_slice_in_dim(kernels[0], core * HALF, HALF, 0)
    mine = mine.reshape(GROUPS, 4, 4, NF, NF).transpose(0, 2, 3, 1, 4).reshape(GROUPS, 4, NF, 4 * NF)
    before = send(mine, 0, 1)
    after = send(mine, 0, -1)
    far = send(mine, 0, 2)
    spectra, heights = analyse(mask_tiles, cell_of_tile)
    low = jnp.stack([mine, after_all(before, heights)])
    high = jnp.stack([after_all(far, heights), after])
    low_before = send(low, 1, 1)
    high_after = send(high, 1, -1)
    high_before = send(high, 1, 1)
    low_after = send(low, 1, -1)
    heights = summed(heights, "tile")
    low_far = send(after_all(low_before, heights), 1, 1)
    high_far = send(after_all(high_after, heights), 1, -1)
    heights = summed(heights, "focus")
    other_spectra = partner(spectra)
    pieces = (low, high, low_before, high_before, low_far, high_far, low_after, high_after)
    other = image(
        place, other_labels[:TILES], other_labels[TILES:], class_center, heights, other_spectra, pieces, BF16
    )
    other = partner(other)
    own = image(place, classes, cell_of_tile, class_center, heights, spectra, pieces, F32)
    return resist(own, other)


def solution(mesh):
    placed = (
        P(("tile", "focus"), None, None),
        P(("tile", "focus"), None),
        P(("tile", "focus")),
        P("focus", None, None, None),
        P(),
    )
    return jax.shard_map(
        device_steps,
        mesh=mesh,
        in_specs=placed,
        out_specs=P(("tile", "focus"), None, None),
        check_vma=False,
    )
```

profile of v0, /device:TPU:1, one launch (start us, length us, event | category | flops | bytes accessed | tf_op | source)
XLA Modules:
  0.0 80.4 jit_solution(5100412549916872254)
XLA Ops:
  0.0 1.1 %copy-done = bf16[1,24,4,4096]{3,2,1,0:T(4,128)(2,1)S(1)} copy-done((bf16[1,24,4,4096]{3,2,1,0:T(4,128)(2,1)S(1)}, bf16[1,24,4,4096]{3,2,1,0:T(4,128)(2,1)}, u32[]{:S(2)}) %copy-start) | copy-done | bytes 786456
  1.1 0.2 constant_dynamic-slice_fusion
  1.3 0.6 reshape.10
  1.9 0.6 copy.18
  2.5 0.5 reshape.11
  3.0 3.6 %collective-permute-start.1 = (bf16[3,4,64,256]{3,2,1,0:T(8,128)(2,1)S(1)}, bf16[3,4,64,256]{3,2,1,0:T(8,128)(2,1)S(1)}, u32[]{:S(2)}, u32[]{:S(2)}) collective-permute-start(bf16[3,4,64,256]{3,2,1,0:T(8,128)(2,1)S(1)} %reshape.11), channel_id=1, source_target_pairs={{0,2},{1,3},{2,0},{3,1},{4,6},{5,7},{6,4},{7,5},{8,10},{9,11},{10,... | collective-permute-start | bytes 1179656 | tf_op jit(solution)/shard_map/ppermute | solution.py:286
  6.7 0.3 collective-permute-start
  7.0 2.4 %collective-permute-start.2 = (bf16[3,4,64,256]{3,2,1,0:T(8,128)(2,1)S(1)}, bf16[3,4,64,256]{3,2,1,0:T(8,128)(2,1)S(1)}, u32[]{:S(2)}, u32[]{:S(2)}) collective-permute-start(bf16[3,4,64,256]{3,2,1,0:T(8,128)(2,1)S(1)} %reshape.11), channel_id=1, source_target_pairs={{0,3},{1,0},{2,1},{3,2},{4,7},{5,4},{6,5},{7,6},{8,11},{9,8},{10,9... | collective-permute-start | bytes 1179656 | tf_op jit(solution)/shard_map/ppermute | solution.py:286
  9.3 0.5 stack_reshape.3
  9.8 0.0 copy-start.4
  9.8 0.0 copy-start.7
  9.8 7.8 %analyse.1 = (bf16[8,2,64,128]{3,2,1,0:T(8,128)(2,1)}, f32[8,128]{1,0:T(8,128)}) custom-call(s32[8]{0:T(128)} %cell_ref.3, bf16[8,512,512]{2,1,0:T(8,128)(2,1)} %mask_hbm.1, bf16[512,128]{1,0:T(8,128)(2,1)} %constant.80.wave_t_ref, bf16[128,512]{1,0:T(8,128)(2,1)} %constant.81.wave_ref, f32[32,8,128]{2,1,0:T(8,128)} %constant.70.clone.row_ref, ...), custom_call_target="tpu_custom_call" | custom-call | flops 1000000000 | bytes 6000000 | tf_op jit(solution)/shard_map/analyse/pallas_call | solution.py:148
  17.6 0.0 collective-permute-done.1
  17.6 0.0 collective-permute-done
  17.6 0.1 pad_maximum_fusion.rest_0_
  17.7 0.0 copy-start.1
  17.7 1.4 %collective-permute-start.3 = (bf16[2,3,4,64,256]{4,3,2,1,0:T(8,128)(2,1)S(1)}, bf16[2,3,4,64,256]{4,3,2,1,0:T(8,128)(2,1)}, u32[]{:S(2)}, u32[]{:S(2)}) collective-permute-start(bf16[2,3,4,64,256]{4,3,2,1,0:T(8,128)(2,1)S(1)} %pad_maximum_fusion.rest_0_), channel_id=1, source_target_pairs={{0,4},{1,5},{2,6},{3,7},{4,8},{5,9},{6,10},{7,11},{8,12},{9,13},{1... | collective-permute-start | bytes 2359304 | tf_op jit(solution)/shard_map/ppermute | solution.py:286
  19.1 0.0 collective-permute-done.2
  19.1 0.1 pad_maximum_fusion.1.rest_1_
  19.2 1.5 %collective-permute-start.6 = (bf16[2,3,4,64,256]{4,3,2,1,0:T(8,128)(2,1)S(1)}, bf16[2,3,4,64,256]{4,3,2,1,0:T(8,128)(2,1)S(1)}, u32[]{:S(2)}, u32[]{:S(2)}) collective-permute-start(bf16[2,3,4,64,256]{4,3,2,1,0:T(8,128)(2,1)S(1)} %pad_maximum_fusion.1.rest_1_), channel_id=1, source_target_pairs={{0,12},{1,13},{2,14},{3,15},{4,0},{5,1},{6,2},{7,3},{8,4},{9,5},{1... | collective-permute-start | bytes 2359304 | tf_op jit(solution)/shard_map/ppermute | solution.py:286
  20.7 0.7 broadcast_in_dim.4
  21.4 12.0 %all_to_all.10 = f32[8,8,128]{2,1,0:T(8,128)S(1)} all-to-all(f32[8,8,128]{2,1,0:T(8,128)S(1)} %broadcast_in_dim.4), channel_id=1, replica_groups=mesh['tile'=8,'focus'=16] {'tile'}, dimensions={0} | all-to-all | bytes 65536 | tf_op jit(solution)/shard_map/all_to_all | solution.py:300
  33.4 0.8 %collective-permute-start.8 = (bf16[2,3,4,64,256]{4,3,2,1,0:T(8,128)(2,1)S(1)}, bf16[2,3,4,64,256]{4,3,2,1,0:T(8,128)(2,1)}, u32[]{:S(2)}, u32[]{:S(2)}) collective-permute-start(bf16[2,3,4,64,256]{4,3,2,1,0:T(8,128)(2,1)S(1)} %pad_maximum_fusion.rest_0_), channel_id=1, source_target_pairs={{0,12},{1,13},{2,14},{3,15},{4,0},{5,1},{6,2},{7,3},{8,4},{9,5},{1... | collective-permute-start | bytes 2359304 | tf_op jit(solution)/shard_map/ppermute | solution.py:286
  34.2 0.6 collective-permute-start.4
  34.8 0.0 collective-permute-done.3.rest_2_
  34.8 0.2 collective-permute-start.5
  35.1 0.0 collective-permute-done.6.rest_7_
  35.1 2.5 %collective-permute-start.7 = (bf16[2,3,4,64,256]{4,3,2,1,0:T(8,128)(2,1)S(1)}, bf16[2,3,4,64,256]{4,3,2,1,0:T(8,128)(2,1)}, u32[]{:S(2)}, u32[]{:S(2)}) collective-permute-start(bf16[2,3,4,64,256]{4,3,2,1,0:T(8,128)(2,1)S(1)} %collective-permute-done.6.rest_7_), channel_id=1, source_target_pairs={{0,12},{1,13},{2,14},{3,15},{4,0},{5,1},{6,2},{7,3},{8,4},{9,5},{1... | collective-permute-start | bytes 2359304 | tf_op jit(solution)/shard_map/ppermute | solution.py:286
  37.5 0.1 pad_add_fusion.1
  37.6 1.9 %collective-permute-start.9 = (s32[16]{0:T(128)S(1)}, s32[16]{0:T(128)S(1)}, u32[]{:S(2)}, u32[]{:S(2)}) collective-permute-start(s32[16]{0:T(128)S(1)} %pad_add_fusion.1), channel_id=1, source_target_pairs={{0,16},{16,0},{32,48},{48,32},{64,80},{80,64},{96,112},{112,96},{1... | collective-permute-start | bytes 200 | tf_op jit(solution)/shard_map/ppermute | solution.py:294
  39.5 0.8 %collective-permute-done.9 = s32[16]{0:T(128)S(1)} collective-permute-done((s32[16]{0:T(128)S(1)}, s32[16]{0:T(128)S(1)}, u32[]{:S(2)}, u32[]{:S(2)}) %collective-permute-start.9) | collective-permute-done | bytes 96 | tf_op jit(solution)/shard_map/ppermute | solution.py:294
  40.3 0.3 collective-permute-start.10
  40.6 0.6 pad_add_fusion.place_ref
  41.2 0.6 broadcast_in_dim.5
  41.9 3.5 %all-to-all-start.1 = ((f32[16,8,128]{2,1,0:T(8,128)}), f32[16,8,128]{2,1,0:T(8,128)S(1)}, u32[]{:S(2)}, u32[]{:S(2)}) async-start(f32[16,8,128]{2,1,0:T(8,128)} %broadcast_in_dim.5), calls=%async_computation.1 | async-start | bytes 131072 | tf_op jit(solution)/shard_map/all_to_all | solution.py:300
  45.4 0.7 fusion
  46.0 9.6 %all-to-all-done.1 = f32[16,8,128]{2,1,0:T(8,128)S(1)} async-done(((f32[16,8,128]{2,1,0:T(8,128)}), f32[16,8,128]{2,1,0:T(8,128)S(1)}, u32[]{:S(2)}, u32[]{:S(2)}) %all-to-all-start.1) | async-done | bytes 65568 | tf_op jit(solution)/shard_map/all_to_all | solution.py:300
  55.6 0.6 reduce_sum.19.height_ref
  56.2 0.0 collective-permute-done.10.spec_ref
  56.2 0.0 collective-permute-done.8.rest_6_
  56.2 0.0 collective-permute-done.4.rest_3_
  56.3 0.0 collective-permute-done.7.rest_5_
  56.3 0.7 copy-done.6
  57.0 7.7 %image.3 = bf16[8,128,128]{2,1,0:T(8,128)(2,1)} custom-call(s32[4]{0:T(128)} %pad_add_fusion.place_ref, s32[8]{0:T(128)} %get-tuple-element.18.class_ref, s32[8]{0:T(128)} %get-tuple-element.17.cell_ref, f32[16]{0:T(128)} %centre_ref.3, f32[8,128]{1,0:T(8,128)} %reduce_sum.19.height_ref, bf16[8,2,64,128]{3,2,1,0:T(8,128)(2,1)} %copy-done.6, ...), custom_call_target="tpu_custom_call" | custom-call | flops 3000000000 | bytes 4000000 | tf_op jit(solution)/shard_map/image/pallas_call | solution.py:232
  64.7 3.0 %collective-permute-start.11 = (bf16[8,128,128]{2,1,0:T(8,128)(2,1)}, bf16[8,128,128]{2,1,0:T(8,128)(2,1)S(1)}, u32[]{:S(2)}, u32[]{:S(2)}) collective-permute-start(bf16[8,128,128]{2,1,0:T(8,128)(2,1)} %image.3), channel_id=1, source_target_pairs={{0,16},{16,0},{32,48},{48,32},{64,80},{80,64},{96,112},{112,96},{1... | collective-permute-start | bytes 786440 | tf_op jit(solution)/shard_map/ppermute | solution.py:294
  67.7 7.8 %image.2.own_ref = f32[8,128,128]{2,1,0:T(8,128)} custom-call(s32[4]{0:T(128)} %pad_add_fusion.place_ref, s32[8]{0:T(128)} %bitcast.13, s32[8]{0:T(128)} %cell_ref.3, f32[16]{0:T(128)} %centre_ref.3, f32[8,128]{1,0:T(8,128)} %reduce_sum.19.height_ref, bf16[8,2,64,128]{3,2,1,0:T(8,128)(2,1)} %get-tuple-element.12.spec_ref, ...), custom_call_target="tpu_custom_call" | custom-call | flops 3000000000 | bytes 4000000 | tf_op jit(solution)/shard_map/image/pallas_call | solution.py:232
  75.5 0.7 copy-done.3
  76.2 4.2 %resist.1 = bf16[8,512,512]{2,1,0:T(8,128)(2,1)} custom-call(f32[8,128,128]{2,1,0:T(8,128)} %image.2.own_ref, bf16[8,128,128]{2,1,0:T(8,128)(2,1)} %copy-done.3, bf16[512,128]{1,0:T(8,128)(2,1)} %constant.84.resist_ref, bf16[128,512]{1,0:T(8,128)(2,1)} %constant.85.resist_t_ref), custom_call_target="tpu_custom_call" | custom-call | flops 1000000000 | bytes 5000000 | tf_op jit(solution)/shard_map/resist/pallas_call | solution.py:258
  (13 shorter events, 0.0 us)
Async XLA Ops:
  0.0 1.1 %copy-start = (bf16[1,24,4,4096]{3,2,1,0:T(4,128)(2,1)S(1)}, bf16[1,24,4,4096]{3,2,1,0:T(4,128)(2,1)}, u32[]{:S(2)}) copy-start(bf16[1,24,4,4096]{3,2,1,0:T(4,128)(2,1)} %param.18) | copy-start | bytes 2359300
  3.0 14.6 %collective-permute-start.1 = (bf16[3,4,64,256]{3,2,1,0:T(8,128)(2,1)S(1)}, bf16[3,4,64,256]{3,2,1,0:T(8,128)(2,1)S(1)}, u32[]{:S(2)}, u32[]{:S(2)}) collective-permute-start(bf16[3,4,64,256]{3,2,1,0:T(8,128)(2,1)S(1)} %reshape.11), channel_id=1, source_target_pairs={{0,2},{1,3},{2,0},{3,1},{4,6},{5,7},{6,4},{7,5},{8,10},{9,11},{10,... | collective-permute-start | bytes 1179656 | tf_op jit(solution)/shard_map/ppermute | solution.py:286
  6.7 11.0 %collective-permute-start = (bf16[3,4,64,256]{3,2,1,0:T(8,128)(2,1)S(1)}, bf16[3,4,64,256]{3,2,1,0:T(8,128)(2,1)S(1)}, u32[]{:S(2)}, u32[]{:S(2)}) collective-permute-start(bf16[3,4,64,256]{3,2,1,0:T(8,128)(2,1)S(1)} %reshape.11), channel_id=1, source_target_pairs={{0,1},{1,2},{2,3},{3,0},{4,5},{5,6},{6,7},{7,4},{8,9},{9,10},{10,1... | collective-permute-start | bytes 1179656 | tf_op jit(solution)/shard_map/ppermute | solution.py:286
  7.0 12.1 %collective-permute-start.2 = (bf16[3,4,64,256]{3,2,1,0:T(8,128)(2,1)S(1)}, bf16[3,4,64,256]{3,2,1,0:T(8,128)(2,1)S(1)}, u32[]{:S(2)}, u32[]{:S(2)}) collective-permute-start(bf16[3,4,64,256]{3,2,1,0:T(8,128)(2,1)S(1)} %reshape.11), channel_id=1, source_target_pairs={{0,3},{1,0},{2,1},{3,2},{4,7},{5,4},{6,5},{7,6},{8,11},{9,8},{10,9... | collective-permute-start | bytes 1179656 | tf_op jit(solution)/shard_map/ppermute | solution.py:286
  9.8 27.7 %copy-start.4 = (s32[8]{0:T(128)S(1)}, s32[8]{0:T(128)}, u32[]{:S(2)}) copy-start(s32[8]{0:T(128)} %cell_ref.3) | copy-start | bytes 100
  9.8 27.7 %copy-start.7 = (s32[8,1]{0,1:T(1,128)S(1)}, s32[8,1]{0,1:T(1,128)}, u32[]{:S(2)}) copy-start(s32[8,1]{0,1:T(1,128)} %param.16) | copy-start | bytes 100
  17.7 38.6 %copy-start.1 = (bf16[2,3,4,64,256]{4,3,2,1,0:T(8,128)(2,1)}, bf16[2,3,4,64,256]{4,3,2,1,0:T(8,128)(2,1)S(1)}, u32[]{:S(2)}) copy-start(bf16[2,3,4,64,256]{4,3,2,1,0:T(8,128)(2,1)S(1)} %pad_maximum_fusion.rest_0_) | copy-start | bytes 2359300
  17.7 17.1 %collective-permute-start.3 = (bf16[2,3,4,64,256]{4,3,2,1,0:T(8,128)(2,1)S(1)}, bf16[2,3,4,64,256]{4,3,2,1,0:T(8,128)(2,1)}, u32[]{:S(2)}, u32[]{:S(2)}) collective-permute-start(bf16[2,3,4,64,256]{4,3,2,1,0:T(8,128)(2,1)S(1)} %pad_maximum_fusion.rest_0_), channel_id=1, source_target_pairs={{0,4},{1,5},{2,6},{3,7},{4,8},{5,9},{6,10},{7,11},{8,12},{9,13},{1... | collective-permute-start | bytes 2359304 | tf_op jit(solution)/shard_map/ppermute | solution.py:286
  19.2 37.1 %copy-start.2 = (bf16[2,3,4,64,256]{4,3,2,1,0:T(8,128)(2,1)}, bf16[2,3,4,64,256]{4,3,2,1,0:T(8,128)(2,1)S(1)}, u32[]{:S(2)}) copy-start(bf16[2,3,4,64,256]{4,3,2,1,0:T(8,128)(2,1)S(1)} %pad_maximum_fusion.1.rest_1_) | copy-start | bytes 2359300
  19.2 15.9 %collective-permute-start.6 = (bf16[2,3,4,64,256]{4,3,2,1,0:T(8,128)(2,1)S(1)}, bf16[2,3,4,64,256]{4,3,2,1,0:T(8,128)(2,1)S(1)}, u32[]{:S(2)}, u32[]{:S(2)}) collective-permute-start(bf16[2,3,4,64,256]{4,3,2,1,0:T(8,128)(2,1)S(1)} %pad_maximum_fusion.1.rest_1_), channel_id=1, source_target_pairs={{0,12},{1,13},{2,14},{3,15},{4,0},{5,1},{6,2},{7,3},{8,4},{9,5},{1... | collective-permute-start | bytes 2359304 | tf_op jit(solution)/shard_map/ppermute | solution.py:286
  33.4 22.9 %collective-permute-start.8 = (bf16[2,3,4,64,256]{4,3,2,1,0:T(8,128)(2,1)S(1)}, bf16[2,3,4,64,256]{4,3,2,1,0:T(8,128)(2,1)}, u32[]{:S(2)}, u32[]{:S(2)}) collective-permute-start(bf16[2,3,4,64,256]{4,3,2,1,0:T(8,128)(2,1)S(1)} %pad_maximum_fusion.rest_0_), channel_id=1, source_target_pairs={{0,12},{1,13},{2,14},{3,15},{4,0},{5,1},{6,2},{7,3},{8,4},{9,5},{1... | collective-permute-start | bytes 2359304 | tf_op jit(solution)/shard_map/ppermute | solution.py:286
  34.2 22.0 %collective-permute-start.4 = (bf16[2,3,4,64,256]{4,3,2,1,0:T(8,128)(2,1)S(1)}, bf16[2,3,4,64,256]{4,3,2,1,0:T(8,128)(2,1)}, u32[]{:S(2)}, u32[]{:S(2)}) collective-permute-start(bf16[2,3,4,64,256]{4,3,2,1,0:T(8,128)(2,1)S(1)} %pad_maximum_fusion.1.rest_1_), channel_id=1, source_target_pairs={{0,4},{1,5},{2,6},{3,7},{4,8},{5,9},{6,10},{7,11},{8,12},{9,13},{1... | collective-permute-start | bytes 2359304 | tf_op jit(solution)/shard_map/ppermute | solution.py:286
  34.8 21.4 %collective-permute-start.5 = (bf16[2,3,4,64,256]{4,3,2,1,0:T(8,128)(2,1)}, bf16[2,3,4,64,256]{4,3,2,1,0:T(8,128)(2,1)}, u32[]{:S(2)}, u32[]{:S(2)}) collective-permute-start(bf16[2,3,4,64,256]{4,3,2,1,0:T(8,128)(2,1)} %collective-permute-done.3.rest_2_), channel_id=1, source_target_pairs={{0,4},{1,5},{2,6},{3,7},{4,8},{5,9},{6,10},{7,11},{8,12},{9,13},{1... | collective-permute-start | bytes 2359304 | tf_op jit(solution)/shard_map/ppermute | solution.py:286
  35.1 21.2 %copy-start.5 = (bf16[2,3,4,64,256]{4,3,2,1,0:T(8,128)(2,1)}, bf16[2,3,4,64,256]{4,3,2,1,0:T(8,128)(2,1)S(1)}, u32[]{:S(2)}) copy-start(bf16[2,3,4,64,256]{4,3,2,1,0:T(8,128)(2,1)S(1)} %collective-permute-done.6.rest_7_) | copy-start | bytes 2359300
  35.1 21.2 %collective-permute-start.7 = (bf16[2,3,4,64,256]{4,3,2,1,0:T(8,128)(2,1)S(1)}, bf16[2,3,4,64,256]{4,3,2,1,0:T(8,128)(2,1)}, u32[]{:S(2)}, u32[]{:S(2)}) collective-permute-start(bf16[2,3,4,64,256]{4,3,2,1,0:T(8,128)(2,1)S(1)} %collective-permute-done.6.rest_7_), channel_id=1, source_target_pairs={{0,12},{1,13},{2,14},{3,15},{4,0},{5,1},{6,2},{7,3},{8,4},{9,5},{1... | collective-permute-start | bytes 2359304 | tf_op jit(solution)/shard_map/ppermute | solution.py:286
  37.6 2.7 %collective-permute-start.9 = (s32[16]{0:T(128)S(1)}, s32[16]{0:T(128)S(1)}, u32[]{:S(2)}, u32[]{:S(2)}) collective-permute-start(s32[16]{0:T(128)S(1)} %pad_add_fusion.1), channel_id=1, source_target_pairs={{0,16},{16,0},{32,48},{48,32},{64,80},{80,64},{96,112},{112,96},{1... | collective-permute-start | bytes 200 | tf_op jit(solution)/shard_map/ppermute | solution.py:294
  40.3 15.9 %collective-permute-start.10 = (bf16[8,2,64,128]{3,2,1,0:T(8,128)(2,1)}, bf16[8,2,64,128]{3,2,1,0:T(8,128)(2,1)S(1)}, u32[]{:S(2)}, u32[]{:S(2)}) collective-permute-start(bf16[8,2,64,128]{3,2,1,0:T(8,128)(2,1)} %get-tuple-element.12.spec_ref), channel_id=1, source_target_pairs={{0,16},{16,0},{32,48},{48,32},{64,80},{80,64},{96,112},{112,96},{1... | collective-permute-start | bytes 786440 | tf_op jit(solution)/shard_map/ppermute | solution.py:294
  41.9 13.8 %all-to-all-start.1 = ((f32[16,8,128]{2,1,0:T(8,128)}), f32[16,8,128]{2,1,0:T(8,128)S(1)}, u32[]{:S(2)}, u32[]{:S(2)}) async-start(f32[16,8,128]{2,1,0:T(8,128)} %broadcast_in_dim.5), calls=%async_computation.1 | async-start | bytes 131072 | tf_op jit(solution)/shard_map/all_to_all | solution.py:300
  56.2 0.7 copy-start.6
  64.7 10.9 %collective-permute-start.11 = (bf16[8,128,128]{2,1,0:T(8,128)(2,1)}, bf16[8,128,128]{2,1,0:T(8,128)(2,1)S(1)}, u32[]{:S(2)}, u32[]{:S(2)}) collective-permute-start(bf16[8,128,128]{2,1,0:T(8,128)(2,1)} %image.3), channel_id=1, source_target_pairs={{0,16},{16,0},{32,48},{48,32},{64,80},{80,64},{96,112},{112,96},{1... | collective-permute-start | bytes 786440 | tf_op jit(solution)/shard_map/ppermute | solution.py:294
  75.5 0.7 copy-start.3
where the time goes:
time: 80.8 us; the launch traced here: 80.4 us
  Pallas kernels  27.5 us (34%)
  starting transfers between devices  22.1 us (27%)
  blocking collectives  12 us (15%)
  waiting for transfers between devices  10.5 us (13%)
  local copies, waits for them, and re-layouts  6.8 us (8%)
  other arithmetic  1.42 us (2%)
    pallas_call x2, Pallas kernels, image(): pl.pallas_call(image_kernel, in_specs=[SMEM] * 4 + [VMEM] * 4 + [ANY] * 8...  15.5 us
    ppermute x9, starting transfers between devices, send(): return lax.ppermute(value, ALL, ring(phase, step))  13.4 us
    all_to_all x1, blocking collectives, summed(): return jnp.sum(lax.all_to_all(copies, axis, 0, 0, tiled=True), axis=0)  12 us
    all_to_all x1, waiting for transfers between devices, summed(): return jnp.sum(lax.all_to_all(copies, axis, 0, 0, tiled=True), axis=0)  9.61 us
    pallas_call x1, Pallas kernels, analyse(): pl.pallas_call(analyse_kernel, in_specs=[SMEM, ANY] + [VMEM] * 4, out_spe...  7.77 us
    ppermute x3, starting transfers between devices, partner(): return lax.ppermute(x, 'tile', [(t, t ^ 1) for t in range(8)])  5.25 us
    pallas_call x1, Pallas kernels, resist(): pl.pallas_call(functools.partial(resist_kernel, count), grid=(TILES // co...  4.18 us
    all_to_all x1, starting transfers between devices, summed(): return jnp.sum(lax.all_to_all(copies, axis, 0, 0, tiled=True), axis=0)  3.49 us
  transfers between devices with their start and end apart: 13, of which 2 were waited for; matrix products, arithmetic and copies ran while one was open for 5% of the time, Pallas kernels for 19%

commit v1 on v0

--- a/solution.py
+++ b/solution.py
@@ -1,5 +1,3 @@
-import functools
-
 import jax
 import jax.numpy as jnp
 import numpy as np
@@ -14,6 +12,7 @@
 KER = 24
 BLK_PX = 64
 SC = 32
+NSUP = 1024
 Q = 128
 B = 8
 REACH = 64
@@ -80,25 +79,32 @@
     return jnp.asarray(table.astype(np.float32)).astype(BF16)
 
 
-def fixed(*shape):
-    return pl.BlockSpec(shape, lambda *_: (0,) * len(shape))
-
-
-def tiles(count, *shape):
-    return pl.BlockSpec((count, *shape), lambda t: (t,) + (0,) * len(shape))
-
-
 SMEM = pl.BlockSpec(memory_space=pltpu.SMEM)
 VMEM = pl.BlockSpec(memory_space=pltpu.VMEM)
 ANY = pl.BlockSpec(memory_space=pl.ANY)
 
 
-def analyse_kernel(cell_ref, mask_hbm, wave_t_ref, wave_ref, row_ref, col_ref, spec_ref, height_ref, mask, rows, along, sems):
+def analyse_kernel(
+    cell_ref, mask_hbm, wave_t_hbm, wave_hbm, row_hbm, col_hbm, spec_ref, height_ref,
+    mask, wave_t_ref, wave_ref, row_ref, col_ref, rows, along, sems, table_sems,
+):
     def copy(t):
         return pltpu.make_async_copy(mask_hbm.at[t], mask.at[t], sems.at[t])
 
-    for t in range(TILES):
+    tables = [
+        pltpu.make_async_copy(source, target, table_sems.at[at])
+        for at, (source, target) in enumerate(
+            ((row_hbm, row_ref), (col_hbm, col_ref), (wave_t_hbm, wave_t_ref), (wave_hbm, wave_ref))
+        )
+    ]
+    for t in range(2):
         copy(t).start()
+    for table in tables:
+        table.start()
+    for t in range(2, TILES):
+        copy(t).start()
+    for table in tables:
+        table.wait()
     lower = lax.broadcasted_iota(jnp.int32, (NF, 2 * NF), 1) < NF
     left = lax.broadcasted_iota(jnp.int32, (B, 2 * BLK_PX), 1) < BLK_PX
     scale = 1.0 / P_SIZE
@@ -147,7 +153,7 @@
     row_part, col_part = height_tables()
     return pl.pallas_call(
         analyse_kernel,
-        in_specs=[SMEM, ANY] + [VMEM] * 4,
+        in_specs=[SMEM] + [ANY] * 5,
         out_specs=[VMEM, VMEM],
         out_shape=[
             jax.ShapeDtypeStruct((TILES, 2, NF, 2 * NF), BF16),
@@ -155,24 +161,39 @@
         ],
         scratch_shapes=[
             pltpu.VMEM((TILES, P_SIZE, P_SIZE), BF16),
+            pltpu.VMEM((P_SIZE, 2 * NF), BF16),
+            pltpu.VMEM((2 * NF, P_SIZE), BF16),
+            pltpu.VMEM((SC, B, 4 * SC), F32),
+            pltpu.VMEM((SC, B, 4 * SC), F32),
             pltpu.VMEM((TILES * B, 4 * SC), F32),
             pltpu.VMEM((TILES * B, 4 * SC), F32),
             pltpu.SemaphoreType.DMA((TILES,)),
+            pltpu.SemaphoreType.DMA((4,)),
         ],
         name="analyse",
+        compiler_params=pltpu.CompilerParams(vmem_limit_bytes=12 << 20),
         cost_estimate=pl.CostEstimate(flops=10**9, bytes_accessed=6 * 10**6, transcendentals=0),
     )(cell_of_tile, mask_tiles, as_bf16(wave.T), as_bf16(wave), jnp.asarray(row_part), jnp.asarray(col_part))
 
 
 def image_kernel(
-    place_ref, class_ref, cell_ref, centre_ref, height_ref, spec_ref, left_ref, pair_ref, *rest
+    first_ref, second_ref, first_div_ref, second_div_ref, label_ref, centre_ref, height_ref,
+    spec_hbm, left_hbm, pair_hbm, *rest
 ):
-    pieces, (out_ref, held, sems) = rest[:8], rest[8:]
+    pieces, (out_ref, held, spec_ref, left_ref, pair_ref, sems, table_sems) = rest[:8], rest[8:]
+    tables = [
+        pltpu.make_async_copy(source, target, table_sems.at[at])
+        for at, (source, target) in enumerate(
+            ((spec_hbm, spec_ref), (left_hbm, left_ref), (pair_hbm, pair_ref))
+        )
+    ]
+    for table in tables:
+        table.start()
 
     def fetch(tile, carry):
-        set_id = class_ref[tile]
-        first = (place_ref[0] - (set_id // place_ref[2])) & 3
-        second = (place_ref[1] - (set_id // place_ref[3])) & 3
+        set_id = label_ref[tile] // NSUP
+        first = (first_ref[0] - (set_id // first_div_ref[0])) & 3
+        second = (second_ref[0] - (set_id // second_div_ref[0])) & 3
         which = second * 2 + first // 2
         for at, ref in enumerate(pieces):
 
@@ -188,16 +209,19 @@
     height_row = lax.broadcasted_iota(jnp.int32, heights.shape, 0)
     height_lane = lax.broadcasted_iota(jnp.int32, heights.shape, 1)
 
+    for table in tables:
+        table.wait()
+
     def some_tiles(trip, carry):
-        batch = [trip * 2, trip * 2 + 1]
+        batch = [trip * 4 + at for at in range(4)]
         for t in batch:
             pltpu.make_async_copy(pieces[0].at[0], held.at[t], sems.at[t]).wait()
         for t in batch:
-            cell = cell_ref[t]
+            cell = label_ref[t] & (NSUP - 1)
             row = cell // SC
             here = (height_row == (row & 7)) & (height_lane == (row // 8) * SC + (cell & (SC - 1)))
             shift = jnp.sum(jnp.where(here, heights, 0.0), keepdims=True) - mean
-            shift = GAIN_SCALE * shift - centre_ref[class_ref[t]]
+            shift = GAIN_SCALE * shift - centre_ref[label_ref[t] // NSUP]
             re_part = spec_ref[t, 0].astype(F32)
             im_part = spec_ref[t, 1].astype(F32)
             re_part = jnp.concatenate([re_part, re_part], axis=1)
@@ -212,56 +236,104 @@
             along = jnp.dot(
                 left_ref[...], jnp.concatenate(filtered, axis=1), preferred_element_type=F32
             ).astype(BF16)
-            both = [
-                jnp.concatenate([along[:Q, at : at + 2 * NF], along[Q:, at : at + 2 * NF]], axis=1)
-                for at in range(0, GROUPS * 4 * NF, 2 * NF)
-            ]
-            fields = jnp.dot(jnp.concatenate(both, axis=0), pair_ref[...], preferred_element_type=F32)
-            total = jnp.zeros((Q, Q), F32)
-            for part in range(4):
-                for at in range(0, GROUPS * 2 * Q, Q):
-                    block = fields[at : at + Q, part * Q : (part + 1) * Q]
-                    total = total + block * block
-            out_ref[t] = total.astype(out_ref.dtype)
+            for rows in range(0, Q, Q // 2):
+                both = [
+                    jnp.concatenate(
+                        [along[rows + half : rows + half + Q // 2, at : at + 2 * NF] for half in (0, Q)],
+                        axis=1,
+                    )
+                    for at in range(0, GROUPS * 4 * NF, 2 * NF)
+                ]
+                fields = jnp.dot(jnp.concatenate(both, axis=0), pair_ref[...], preferred_element_type=F32)
+                total = jnp.zeros((Q // 2, Q), F32)
+                for at in range(0, GROUPS * Q, Q // 2):
+                    for part in range(4):
+                        block = fields[at : at + Q // 2, part * Q : (part + 1) * Q]
+                        total = total + block * block
+                out_ref[t, rows : rows + Q // 2] = total.astype(out_ref.dtype)
         return carry
 
-    lax.fori_loop(0, TILES // 2, some_tiles, 0)
-
-
-def image(place, classes, cells, centre, heights, spectra, pieces, dtype):
+    lax.fori_loop(0, TILES // 4, some_tiles, 0)
+
+
+def image(place, labels, centre, heights, spectra, pieces):
     return pl.pallas_call(
         image_kernel,
-        in_specs=[SMEM] * 4 + [VMEM] * 4 + [ANY] * 8,
+        in_specs=[SMEM] * 6 + [VMEM] + [ANY] * 11,
         out_specs=VMEM,
-        out_shape=jax.ShapeDtypeStruct((TILES, Q, Q), dtype),
+        out_shape=jax.ShapeDtypeStruct((TILES, Q, Q), BF16),
         scratch_shapes=[
             pltpu.VMEM((TILES, GROUPS, 4, NF, 4 * NF), BF16),
+            pltpu.VMEM((TILES, 2, NF, 2 * NF), BF16),
+            pltpu.VMEM((2 * Q, 2 * NF), BF16),
+            pltpu.VMEM((4 * NF, 4 * Q), BF16),
+            pltpu.SemaphoreType.DMA((TILES,)),
+            pltpu.SemaphoreType.DMA((3,)),
+        ],
+        name="image",
+        compiler_params=pltpu.CompilerParams(vmem_limit_bytes=16 << 20),
+        cost_estimate=pl.CostEstimate(flops=3 * 10**9, bytes_accessed=4 * 10**6, transcendentals=0),
+    )(*place, labels, centre, heights, spectra, as_bf16(left_table()), as_bf16(pair_table()), *pieces)
+
+
+def resist_kernel(
+    own_hbm, other_hbm, resist_hbm, resist_t_hbm, out_hbm,
+    own_ref, other_ref, resist_ref, resist_t_ref, image_ref, sems, out_sems,
+):
+    copies = [
+        pltpu.make_async_copy(source, target, sems.at[at])
+        for at, (source, target) in enumerate(
+            (
+                (own_hbm, own_ref),
+                (other_hbm, other_ref),
+                (resist_t_hbm, resist_t_ref),
+                (resist_hbm, resist_ref),
+            )
+        )
+    ]
+    for copy in copies:
+        copy.start()
+    for copy in copies:
+        copy.wait()
+
+    def some_tiles(trip, carry):
+        at = pl.ds(trip * 2, 2)
+        intensity = (own_ref[at].astype(F32) + other_ref[at].astype(F32)) * (1.0 / KER)
+        intensity = intensity.astype(BF16).reshape(2 * Q, Q)
+        half_way = jnp.dot(intensity, resist_t_ref[...], preferred_element_type=F32).astype(BF16)
+        for t in range(2):
+            image_ref[trip * 2 + t] = jnp.dot(
+                resist_ref[...], half_way[t * Q : (t + 1) * Q], preferred_element_type=F32
+            ).astype(BF16)
+            out_copy(trip * 2 + t).start()
+        return carry
+
+    def out_copy(t):
+        return pltpu.make_async_copy(image_ref.at[t], out_hbm.at[t], out_sems.at[t])
+
+    lax.fori_loop(0, TILES // 2, some_tiles, 0)
+    for t in range(TILES):
+        out_copy(t).wait()
+
+
+def resist(own, other):
+    table = resist_table(P_SIZE, Q)
+    return pl.pallas_call(
+        resist_kernel,
+        in_specs=[ANY] * 4,
+        out_specs=ANY,
+        out_shape=jax.ShapeDtypeStruct((TILES, P_SIZE, P_SIZE), BF16),
+        scratch_shapes=[
+            pltpu.VMEM((TILES, Q, Q), BF16),
+            pltpu.VMEM((TILES, Q, Q), BF16),
+            pltpu.VMEM((P_SIZE, Q), BF16),
+            pltpu.VMEM((Q, P_SIZE), BF16),
+            pltpu.VMEM((TILES, P_SIZE, P_SIZE), BF16),
+            pltpu.SemaphoreType.DMA((4,)),
             pltpu.SemaphoreType.DMA((TILES,)),
         ],
-        name="image",
-        cost_estimate=pl.CostEstimate(flops=3 * 10**9, bytes_accessed=4 * 10**6, transcendentals=0),
-    )(place, classes, cells, centre, heights, spectra, as_bf16(left_table()), as_bf16(pair_table()), *pieces)
-
-
-def resist_kernel(count, own_ref, other_ref, resist_ref, resist_t_ref, out_ref):
-    intensity = (own_ref[...] + other_ref[...].astype(F32)) * (1.0 / KER)
-    intensity = intensity.astype(BF16).reshape(count * Q, Q)
-    half_way = jnp.dot(intensity, resist_t_ref[...], preferred_element_type=F32).astype(BF16)
-    for t in range(count):
-        out_ref[t] = jnp.dot(
-            resist_ref[...], half_way[t * Q : (t + 1) * Q], preferred_element_type=F32
-        ).astype(BF16)
-
-
-def resist(own, other, count=4):
-    table = resist_table(P_SIZE, Q)
-    return pl.pallas_call(
-        functools.partial(resist_kernel, count),
-        grid=(TILES // count,),
-        in_specs=[tiles(count, Q, Q), tiles(count, Q, Q), fixed(P_SIZE, Q), fixed(Q, P_SIZE)],
-        out_specs=tiles(count, P_SIZE, P_SIZE),
-        out_shape=jax.ShapeDtypeStruct((TILES, P_SIZE, P_SIZE), BF16),
         name="resist",
+        compiler_params=pltpu.CompilerParams(vmem_limit_bytes=12 << 20),
         cost_estimate=pl.CostEstimate(flops=10**9, bytes_accessed=5 * 10**6, transcendentals=0),
     )(own, other, as_bf16(table), as_bf16(table.T))
 
@@ -304,16 +376,17 @@
     core = lax.axis_index("tile") % 2
     focus = lax.axis_index("focus")
     x, y = focus // 4, focus % 4
-    place = jnp.stack(
-        [
+    place = [
+        jnp.reshape(value.astype(jnp.int32), (1,))
+        for value in (
             jnp.where(core == 0, y, x),
             jnp.where(core == 0, x, y),
             jnp.where(core == 0, 1, 4),
             jnp.where(core == 0, 4, 1),
-        ]
-    ).astype(jnp.int32)
-    classes = class_of_tile[:, 0]
-    other_labels = partner(jnp.concatenate([classes, cell_of_tile]))
+        )
+    ]
+    labels = class_of_tile[:, 0] * NSUP + cell_of_tile
+    other_labels = partner(labels)
 
     mine = lax.dynamic_slice_in_dim(kernels[0], core * HALF, HALF, 0)
     mine = mine.reshape(GROUPS, 4, 4, NF, NF).transpose(0, 2, 3, 1, 4).reshape(GROUPS, 4, NF, 4 * NF)
@@ -333,11 +406,9 @@
     heights = summed(heights, "focus")
     other_spectra = partner(spectra)
     pieces = (low, high, low_before, high_before, low_far, high_far, low_after, high_after)
-    other = image(
-        place, other_labels[:TILES], other_labels[TILES:], class_center, heights, other_spectra, pieces, BF16
-    )
+    other = image(place, other_labels, class_center, heights, other_spectra, pieces)
     other = partner(other)
-    own = image(place, classes, cell_of_tile, class_center, heights, spectra, pieces, F32)
+    own = image(place, labels, class_center, heights, spectra, pieces)
     return resist(own, other)
 
 

time: 80.8 us -> 77.3 us (0.957)
  Pallas kernels: 27.5 us -> 22.2 us
  local copies, waits for them, and re-layouts: 6.8 us -> 7.98 us
    pallas_call x4, Pallas kernels: 27.5 us -> 22.2 us  [the longest x2 12.1 us: image(): pl.pallas_call(image_kernel, in_specs=[SMEM] * 6 + [VMEM] + [ANY] * 11, o...]
    unnamed x16 -> x26, local copies, waits for them, and re-layouts: 2.51 us -> 4.25 us
    another operation x1, other arithmetic: 0.07 us -> 1.19 us  [device_steps(): high = jnp.stack([after_all(far, heights), after])]
  transfers between devices with their start and end apart: 13 -> 13, of which waited for: 2 -> 2; matrix products, arithmetic and copies ran while one was open for 5% -> 3% of each run, Pallas kernels for 19% -> 16%
where the time goes in v1:
time: 77.3 us; the launch traced here: 76.9 us
  Pallas kernels  22.2 us (29%)
  starting transfers between devices  22 us (28%)
  blocking collectives  12 us (16%)
  waiting for transfers between devices  11.2 us (14%)
  local copies, waits for them, and re-layouts  7.98 us (10%)
  other arithmetic  1.3 us (2%)
    ppermute x9, starting transfers between devices, send(): return lax.ppermute(value, ALL, ring(phase, step))  13.3 us
    pallas_call x2, Pallas kernels, image(): pl.pallas_call(image_kernel, in_specs=[SMEM] * 6 + [VMEM] + [ANY] * 11, o...  12.1 us
    all_to_all x1, blocking collectives, summed(): return jnp.sum(lax.all_to_all(copies, axis, 0, 0, tiled=True), axis=0)  12 us
    all_to_all x1, waiting for transfers between devices, summed(): return jnp.sum(lax.all_to_all(copies, axis, 0, 0, tiled=True), axis=0)  10.3 us
    pallas_call x1, Pallas kernels, analyse(): pl.pallas_call(analyse_kernel, in_specs=[SMEM] + [ANY] * 5, out_specs=[VM...  6.43 us
    ppermute x3, starting transfers between devices, partner(): return lax.ppermute(x, 'tile', [(t, t ^ 1) for t in range(8)])  5.21 us
    unnamed x26, local copies, waits for them, and re-layouts  4.25 us
    pallas_call x1, Pallas kernels, resist(): pl.pallas_call(resist_kernel, in_specs=[ANY] * 4, out_specs=ANY, out_shap...  3.63 us
  transfers between devices with their start and end apart: 13, of which 2 were waited for; matrix products, arithmetic and copies ran while one was open for 3% of the time, Pallas kernels for 16%

profile of v1, /device:TPU:1, one launch (start us, length us, event | category | flops | bytes accessed | tf_op | source)
XLA Modules:
  0.0 76.9 jit_solution(1453495784156258814)
XLA Ops:
  0.0 0.0 copy-start.6
  0.0 0.0 copy-start.7
  0.1 1.1 %copy-done = bf16[1,24,4,4096]{3,2,1,0:T(4,128)(2,1)S(1)} copy-done((bf16[1,24,4,4096]{3,2,1,0:T(4,128)(2,1)S(1)}, bf16[1,24,4,4096]{3,2,1,0:T(4,128)(2,1)}, u32[]{:S(2)}) %copy-start) | copy-done | bytes 786456
  1.1 0.2 constant_dynamic-slice_fusion
  1.3 0.6 reshape.28
  1.9 0.6 copy.18
  2.5 1.2 %reshape.29 = bf16[3,4,64,256]{3,2,1,0:T(8,128)(2,1)} reshape(bf16[3,4,64,4,64]{4,3,2,1,0:T(4,128)(2,1)S(1)} %copy.18) | data formatting | bytes 786432 | tf_op jit(solution)/shard_map/reshape | solution.py:392
  3.8 3.6 %collective-permute-start.1 = (bf16[3,4,64,256]{3,2,1,0:T(8,128)(2,1)}, bf16[3,4,64,256]{3,2,1,0:T(8,128)(2,1)}, u32[]{:S(2)}, u32[]{:S(2)}) collective-permute-start(bf16[3,4,64,256]{3,2,1,0:T(8,128)(2,1)} %reshape.29), channel_id=1, source_target_pairs={{0,2},{1,3},{2,0},{3,1},{4,6},{5,7},{6,4},{7,5},{8,10},{9,11},{10,... | collective-permute-start | bytes 1179656 | tf_op jit(solution)/shard_map/ppermute | solution.py:358
  7.3 0.3 collective-permute-start
  7.6 2.4 %collective-permute-start.2 = (bf16[3,4,64,256]{3,2,1,0:T(8,128)(2,1)}, bf16[3,4,64,256]{3,2,1,0:T(8,128)(2,1)}, u32[]{:S(2)}, u32[]{:S(2)}) collective-permute-start(bf16[3,4,64,256]{3,2,1,0:T(8,128)(2,1)} %reshape.29), channel_id=1, source_target_pairs={{0,3},{1,0},{2,1},{3,2},{4,7},{5,4},{6,5},{7,6},{8,11},{9,8},{10,9... | collective-permute-start | bytes 1179656 | tf_op jit(solution)/shard_map/ppermute | solution.py:358
  10.0 0.5 stack_reshape.3
  10.5 0.0 copy-start.1
  10.6 2.2 %copy-done.1 = bf16[8,512,512]{2,1,0:T(8,128)(2,1)S(1)} copy-done((bf16[8,512,512]{2,1,0:T(8,128)(2,1)S(1)}, bf16[8,512,512]{2,1,0:T(8,128)(2,1)}, u32[]{:S(2)}) %copy-start.1) | copy-done | bytes 4194328
  12.7 6.4 %analyse.1 = (bf16[8,2,64,128]{3,2,1,0:T(8,128)(2,1)S(1)}, f32[8,128]{1,0:T(8,128)S(1)}) custom-call(s32[8]{0:T(128)S(1)} %copy-done.8, bf16[8,512,512]{2,1,0:T(8,128)(2,1)S(1)} %copy-done.1, bf16[512,128]{1,0:T(8,128)(2,1)S(1)} %copy-done.5, bf16[128,512]{1,0:T(8,128)(2,1)S(1)} %copy-done.4, f32[32,8,128]{2,1,0:T(8,128)S(1)} %copy-done.7, ...), custom_call_target="tpu_custom_call" | custom-call | flops 1000000000 | bytes 6000000 | tf_op jit(solution)/shard_map/analyse/pallas_call | solution.py:154
  19.2 0.0 collective-permute-done.1
  19.2 0.0 collective-permute-done
  19.2 0.1 pad_maximum_fusion.rest_0_
  19.3 1.4 %collective-permute-start.3 = (bf16[2,3,4,64,256]{4,3,2,1,0:T(8,128)(2,1)S(1)}, bf16[2,3,4,64,256]{4,3,2,1,0:T(8,128)(2,1)S(1)}, u32[]{:S(2)}, u32[]{:S(2)}) collective-permute-start(bf16[2,3,4,64,256]{4,3,2,1,0:T(8,128)(2,1)S(1)} %pad_maximum_fusion.rest_0_), channel_id=1, source_target_pairs={{0,4},{1,5},{2,6},{3,7},{4,8},{5,9},{6,10},{7,11},{8,12},{9,13},{1... | collective-permute-start | bytes 2359304 | tf_op jit(solution)/shard_map/ppermute | solution.py:358
  20.6 0.0 collective-permute-done.2
  20.7 1.2 %pad_maximum_fusion.1.rest_1_ = bf16[2,3,4,64,256]{4,3,2,1,0:T(8,128)(2,1)S(1)} fusion(bf16[1,3,4,64,256]{4,3,2,1,0:T(8,128)(2,1)} %bitcast.8, bf16[1,3,4,64,256]{4,3,2,1,0:T(8,128)(2,1)} %bitcast.7), kind=kLoop, calls=%fused_computation.1 | loop fusion | flops 393216 | bytes 1572864 | tf_op jit(solution)/shard_map/stack | solution.py:398
  21.8 1.5 %collective-permute-start.6 = (bf16[2,3,4,64,256]{4,3,2,1,0:T(8,128)(2,1)S(1)}, bf16[2,3,4,64,256]{4,3,2,1,0:T(8,128)(2,1)}, u32[]{:S(2)}, u32[]{:S(2)}) collective-permute-start(bf16[2,3,4,64,256]{4,3,2,1,0:T(8,128)(2,1)S(1)} %pad_maximum_fusion.1.rest_1_), channel_id=1, source_target_pairs={{0,12},{1,13},{2,14},{3,15},{4,0},{5,1},{6,2},{7,3},{8,4},{9,5},{1... | collective-permute-start | bytes 2359304 | tf_op jit(solution)/shard_map/ppermute | solution.py:358
  23.4 12.0 %all_to_all.10 = f32[8,8,128]{2,1,0:T(8,128)S(1)} all-to-all(f32[8,8,128]{2,1,0:T(8,128)S(1)} %broadcast_in_dim.4), channel_id=1, replica_groups=mesh['tile'=8,'focus'=16] {'tile'}, dimensions={0} | all-to-all | bytes 65536 | tf_op jit(solution)/shard_map/all_to_all | solution.py:372
  35.4 0.3 collective-permute-start.8
  35.7 1.2 %collective-permute-start.4 = (bf16[2,3,4,64,256]{4,3,2,1,0:T(8,128)(2,1)S(1)}, bf16[2,3,4,64,256]{4,3,2,1,0:T(8,128)(2,1)}, u32[]{:S(2)}, u32[]{:S(2)}) collective-permute-start(bf16[2,3,4,64,256]{4,3,2,1,0:T(8,128)(2,1)S(1)} %pad_maximum_fusion.1.rest_1_), channel_id=1, source_target_pairs={{0,4},{1,5},{2,6},{3,7},{4,8},{5,9},{6,10},{7,11},{8,12},{9,13},{1... | collective-permute-start | bytes 2359304 | tf_op jit(solution)/shard_map/ppermute | solution.py:358
  36.8 0.0 collective-permute-done.3.rest_2_
  36.8 0.0 collective-permute-start.5
  36.9 0.0 collective-permute-done.6.rest_7_
  36.9 2.7 %collective-permute-start.7 = (bf16[2,3,4,64,256]{4,3,2,1,0:T(8,128)(2,1)}, bf16[2,3,4,64,256]{4,3,2,1,0:T(8,128)(2,1)}, u32[]{:S(2)}, u32[]{:S(2)}) collective-permute-start(bf16[2,3,4,64,256]{4,3,2,1,0:T(8,128)(2,1)} %collective-permute-done.6.rest_7_), channel_id=1, source_target_pairs={{0,12},{1,13},{2,14},{3,15},{4,0},{5,1},{6,2},{7,3},{8,4},{9,5},{1... | collective-permute-start | bytes 2359304 | tf_op jit(solution)/shard_map/ppermute | solution.py:358
  39.5 1.9 %collective-permute-start.9 = (s32[8]{0:T(128)S(1)}, s32[8]{0:T(128)S(1)}, u32[]{:S(2)}, u32[]{:S(2)}) collective-permute-start(s32[8]{0:T(128)S(1)} %bitcast_add_fusion.label_ref), channel_id=1, source_target_pairs={{0,16},{16,0},{32,48},{48,32},{64,80},{80,64},{96,112},{112,96},{1... | collective-permute-start | bytes 104 | tf_op jit(solution)/shard_map/ppermute | solution.py:366
  41.4 0.8 %collective-permute-done.9.label_ref = s32[8]{0:T(128)S(1)} collective-permute-done((s32[8]{0:T(128)S(1)}, s32[8]{0:T(128)S(1)}, u32[]{:S(2)}, u32[]{:S(2)}) %collective-permute-start.9) | collective-permute-done | bytes 64 | tf_op jit(solution)/shard_map/ppermute | solution.py:366
  42.2 0.3 collective-permute-start.10
  42.5 0.6 broadcast_in_dim.5
  43.2 3.5 %all-to-all-start.1 = ((f32[16,8,128]{2,1,0:T(8,128)}), f32[16,8,128]{2,1,0:T(8,128)S(1)}, u32[]{:S(2)}, u32[]{:S(2)}) async-start(f32[16,8,128]{2,1,0:T(8,128)} %broadcast_in_dim.5), calls=%async_computation.1 | async-start | bytes 131072 | tf_op jit(solution)/shard_map/all_to_all | solution.py:372
  46.7 10.3 %all-to-all-done.1 = f32[16,8,128]{2,1,0:T(8,128)S(1)} async-done(((f32[16,8,128]{2,1,0:T(8,128)}), f32[16,8,128]{2,1,0:T(8,128)S(1)}, u32[]{:S(2)}, u32[]{:S(2)}) %all-to-all-start.1) | async-done | bytes 65568 | tf_op jit(solution)/shard_map/all_to_all | solution.py:372
  57.1 0.0 collective-permute-done.10.spec_hbm
  57.1 0.0 collective-permute-done.8.rest_6_
  57.1 0.0 collective-permute-done.4.rest_3_
  57.1 0.0 collective-permute-done.5.rest_4_
  57.1 0.0 collective-permute-done.7.rest_5_
  57.1 0.0 copy-start.10
  57.2 0.9 %copy-done.10 = bf16[256,512]{1,0:T(8,128)(2,1)S(1)} copy-done((bf16[256,512]{1,0:T(8,128)(2,1)S(1)}, bf16[256,512]{1,0:T(8,128)(2,1)}, u32[]{:S(2)}) %copy-start.10) | copy-done | bytes 262168
  58.1 6.0 %image.3 = bf16[8,128,128]{2,1,0:T(8,128)(2,1)S(1)} custom-call(s32[1]{0:T(128)} %bitcast.first_ref, s32[1]{0:T(128)} %bitcast.1.second_ref, s32[1]{0:T(128)} %bitcast.2.first_div_ref, s32[1]{0:T(128)} %bitcast.3.second_div_ref, s32[8]{0:T(128)S(1)} %collective-permute-done.9.label_ref, f32[16]{0:T(128)S(1)} %copy-done.9, ...), custom_call_target="tpu_custom_call" | custom-call | flops 3000000000 | bytes 4000000 | tf_op jit(solution)/shard_map/image/pallas_call | solution.py:260
  64.1 0.0 copy-start.2
  64.1 0.0 copy-start.3
  64.1 3.0 %collective-permute-start.11 = (bf16[8,128,128]{2,1,0:T(8,128)(2,1)S(1)}, bf16[8,128,128]{2,1,0:T(8,128)(2,1)S(1)}, u32[]{:S(2)}, u32[]{:S(2)}) collective-permute-start(bf16[8,128,128]{2,1,0:T(8,128)(2,1)S(1)} %image.3), channel_id=1, source_target_pairs={{0,16},{16,0},{32,48},{48,32},{64,80},{80,64},{96,112},{112,96},{1... | collective-permute-start | bytes 786440 | tf_op jit(solution)/shard_map/ppermute | solution.py:366
  67.1 6.1 %image.2.own_hbm = bf16[8,128,128]{2,1,0:T(8,128)(2,1)S(1)} custom-call(s32[1]{0:T(128)} %bitcast.first_ref, s32[1]{0:T(128)} %bitcast.1.second_ref, s32[1]{0:T(128)} %bitcast.2.first_div_ref, s32[1]{0:T(128)} %bitcast.3.second_div_ref, s32[8]{0:T(128)S(1)} %bitcast_add_fusion.label_ref, f32[16]{0:T(128)S(1)} %copy-done.9, ...), custom_call_target="tpu_custom_call" | custom-call | flops 3000000000 | bytes 4000000 | tf_op jit(solution)/shard_map/image/pallas_call | solution.py:260
  73.3 0.0 collective-permute-done.11.other_hbm
  73.3 3.6 %resist.1 = bf16[8,512,512]{2,1,0:T(8,128)(2,1)} custom-call(bf16[8,128,128]{2,1,0:T(8,128)(2,1)S(1)} %image.2.own_hbm, bf16[8,128,128]{2,1,0:T(8,128)(2,1)S(1)} %collective-permute-done.11.other_hbm, bf16[512,128]{1,0:T(8,128)(2,1)S(1)} %copy-done.3, bf16[128,512]{1,0:T(8,128)(2,1)S(1)} %copy-done.2), custom_call_target="tpu_custom_call" | custom-call | flops 1000000000 | bytes 5000000 | tf_op jit(solution)/shard_map/resist/pallas_call | solution.py:321
  (21 shorter events, 0.1 us)
Async XLA Ops:
  0.0 1.1 %copy-start = (bf16[1,24,4,4096]{3,2,1,0:T(4,128)(2,1)S(1)}, bf16[1,24,4,4096]{3,2,1,0:T(4,128)(2,1)}, u32[]{:S(2)}) copy-start(bf16[1,24,4,4096]{3,2,1,0:T(4,128)(2,1)} %param.18) | copy-start | bytes 2359300
  0.0 10.5 %copy-start.4 = (bf16[128,512]{1,0:T(8,128)(2,1)S(1)}, bf16[128,512]{1,0:T(8,128)(2,1)}, u32[]{:S(2)}) copy-start(bf16[128,512]{1,0:T(8,128)(2,1)} %constant.83.wave_hbm) | copy-start | bytes 393220
  0.0 10.5 %copy-start.5 = (bf16[512,128]{1,0:T(8,128)(2,1)S(1)}, bf16[512,128]{1,0:T(8,128)(2,1)}, u32[]{:S(2)}) copy-start(bf16[512,128]{1,0:T(8,128)(2,1)} %constant.82.wave_t_hbm) | copy-start | bytes 393220
  0.0 10.5 %copy-start.6 = (f32[32,8,128]{2,1,0:T(8,128)S(1)}, f32[32,8,128]{2,1,0:T(8,128)}, u32[]{:S(2)}) copy-start(f32[32,8,128]{2,1,0:T(8,128)} %constant.73.clone.col_hbm) | copy-start | bytes 393220
  0.0 10.5 %copy-start.7 = (f32[32,8,128]{2,1,0:T(8,128)S(1)}, f32[32,8,128]{2,1,0:T(8,128)}, u32[]{:S(2)}) copy-start(f32[32,8,128]{2,1,0:T(8,128)} %constant.72.clone.row_hbm) | copy-start | bytes 393220
  0.0 10.5 %copy-start.8 = (s32[8]{0:T(128)S(1)}, s32[8]{0:T(128)}, u32[]{:S(2)}) copy-start(s32[8]{0:T(128)} %cell_ref.1) | copy-start | bytes 100
  3.8 15.4 %collective-permute-start.1 = (bf16[3,4,64,256]{3,2,1,0:T(8,128)(2,1)}, bf16[3,4,64,256]{3,2,1,0:T(8,128)(2,1)}, u32[]{:S(2)}, u32[]{:S(2)}) collective-permute-start(bf16[3,4,64,256]{3,2,1,0:T(8,128)(2,1)} %reshape.29), channel_id=1, source_target_pairs={{0,2},{1,3},{2,0},{3,1},{4,6},{5,7},{6,4},{7,5},{8,10},{9,11},{10,... | collective-permute-start | bytes 1179656 | tf_op jit(solution)/shard_map/ppermute | solution.py:358
  7.3 11.9 %collective-permute-start = (bf16[3,4,64,256]{3,2,1,0:T(8,128)(2,1)}, bf16[3,4,64,256]{3,2,1,0:T(8,128)(2,1)S(1)}, u32[]{:S(2)}, u32[]{:S(2)}) collective-permute-start(bf16[3,4,64,256]{3,2,1,0:T(8,128)(2,1)} %reshape.29), channel_id=1, source_target_pairs={{0,1},{1,2},{2,3},{3,0},{4,5},{5,6},{6,7},{7,4},{8,9},{9,10},{10,1... | collective-permute-start | bytes 1179656 | tf_op jit(solution)/shard_map/ppermute | solution.py:358
  7.6 13.0 %collective-permute-start.2 = (bf16[3,4,64,256]{3,2,1,0:T(8,128)(2,1)}, bf16[3,4,64,256]{3,2,1,0:T(8,128)(2,1)}, u32[]{:S(2)}, u32[]{:S(2)}) collective-permute-start(bf16[3,4,64,256]{3,2,1,0:T(8,128)(2,1)} %reshape.29), channel_id=1, source_target_pairs={{0,3},{1,0},{2,1},{3,2},{4,7},{5,4},{6,5},{7,6},{8,11},{9,8},{10,9... | collective-permute-start | bytes 1179656 | tf_op jit(solution)/shard_map/ppermute | solution.py:358
  10.5 2.2 %copy-start.1 = (bf16[8,512,512]{2,1,0:T(8,128)(2,1)S(1)}, bf16[8,512,512]{2,1,0:T(8,128)(2,1)}, u32[]{:S(2)}) copy-start(bf16[8,512,512]{2,1,0:T(8,128)(2,1)} %mask_hbm.1) | copy-start | bytes 12582916
  12.7 26.8 %copy-start.12 = (s32[8,1]{0,1:T(1,128)S(1)}, s32[8,1]{0,1:T(1,128)}, u32[]{:S(2)}) copy-start(s32[8,1]{0,1:T(1,128)} %param.16) | copy-start | bytes 100
  12.7 44.4 %copy-start.9 = (f32[16]{0:T(128)S(1)}, f32[16]{0:T(128)}, u32[]{:S(2)}) copy-start(f32[16]{0:T(128)} %centre_ref.3) | copy-start | bytes 196
  12.7 44.4 %copy-start.11 = (bf16[256,128]{1,0:T(8,128)(2,1)S(1)}, bf16[256,128]{1,0:T(8,128)(2,1)}, u32[]{:S(2)}) copy-start(bf16[256,128]{1,0:T(8,128)(2,1)} %constant.84.left_hbm) | copy-start | bytes 196612
  19.3 17.5 %collective-permute-start.3 = (bf16[2,3,4,64,256]{4,3,2,1,0:T(8,128)(2,1)S(1)}, bf16[2,3,4,64,256]{4,3,2,1,0:T(8,128)(2,1)S(1)}, u32[]{:S(2)}, u32[]{:S(2)}) collective-permute-start(bf16[2,3,4,64,256]{4,3,2,1,0:T(8,128)(2,1)S(1)} %pad_maximum_fusion.rest_0_), channel_id=1, source_target_pairs={{0,4},{1,5},{2,6},{3,7},{4,8},{5,9},{6,10},{7,11},{8,12},{9,13},{1... | collective-permute-start | bytes 2359304 | tf_op jit(solution)/shard_map/ppermute | solution.py:358
  21.8 15.0 %collective-permute-start.6 = (bf16[2,3,4,64,256]{4,3,2,1,0:T(8,128)(2,1)S(1)}, bf16[2,3,4,64,256]{4,3,2,1,0:T(8,128)(2,1)}, u32[]{:S(2)}, u32[]{:S(2)}) collective-permute-start(bf16[2,3,4,64,256]{4,3,2,1,0:T(8,128)(2,1)S(1)} %pad_maximum_fusion.1.rest_1_), channel_id=1, source_target_pairs={{0,12},{1,13},{2,14},{3,15},{4,0},{5,1},{6,2},{7,3},{8,4},{9,5},{1... | collective-permute-start | bytes 2359304 | tf_op jit(solution)/shard_map/ppermute | solution.py:358
  35.4 21.7 %collective-permute-start.8 = (bf16[2,3,4,64,256]{4,3,2,1,0:T(8,128)(2,1)S(1)}, bf16[2,3,4,64,256]{4,3,2,1,0:T(8,128)(2,1)}, u32[]{:S(2)}, u32[]{:S(2)}) collective-permute-start(bf16[2,3,4,64,256]{4,3,2,1,0:T(8,128)(2,1)S(1)} %pad_maximum_fusion.rest_0_), channel_id=1, source_target_pairs={{0,12},{1,13},{2,14},{3,15},{4,0},{5,1},{6,2},{7,3},{8,4},{9,5},{1... | collective-permute-start | bytes 2359304 | tf_op jit(solution)/shard_map/ppermute | solution.py:358
  35.7 21.4 %collective-permute-start.4 = (bf16[2,3,4,64,256]{4,3,2,1,0:T(8,128)(2,1)S(1)}, bf16[2,3,4,64,256]{4,3,2,1,0:T(8,128)(2,1)}, u32[]{:S(2)}, u32[]{:S(2)}) collective-permute-start(bf16[2,3,4,64,256]{4,3,2,1,0:T(8,128)(2,1)S(1)} %pad_maximum_fusion.1.rest_1_), channel_id=1, source_target_pairs={{0,4},{1,5},{2,6},{3,7},{4,8},{5,9},{6,10},{7,11},{8,12},{9,13},{1... | collective-permute-start | bytes 2359304 | tf_op jit(solution)/shard_map/ppermute | solution.py:358
  36.8 20.3 %collective-permute-start.5 = (bf16[2,3,4,64,256]{4,3,2,1,0:T(8,128)(2,1)S(1)}, bf16[2,3,4,64,256]{4,3,2,1,0:T(8,128)(2,1)}, u32[]{:S(2)}, u32[]{:S(2)}) collective-permute-start(bf16[2,3,4,64,256]{4,3,2,1,0:T(8,128)(2,1)S(1)} %collective-permute-done.3.rest_2_), channel_id=1, source_target_pairs={{0,4},{1,5},{2,6},{3,7},{4,8},{5,9},{6,10},{7,11},{8,12},{9,13},{1... | collective-permute-start | bytes 2359304 | tf_op jit(solution)/shard_map/ppermute | solution.py:358
  36.9 20.3 %collective-permute-start.7 = (bf16[2,3,4,64,256]{4,3,2,1,0:T(8,128)(2,1)}, bf16[2,3,4,64,256]{4,3,2,1,0:T(8,128)(2,1)}, u32[]{:S(2)}, u32[]{:S(2)}) collective-permute-start(bf16[2,3,4,64,256]{4,3,2,1,0:T(8,128)(2,1)} %collective-permute-done.6.rest_7_), channel_id=1, source_target_pairs={{0,12},{1,13},{2,14},{3,15},{4,0},{5,1},{6,2},{7,3},{8,4},{9,5},{1... | collective-permute-start | bytes 2359304 | tf_op jit(solution)/shard_map/ppermute | solution.py:358
  39.5 2.7 %collective-permute-start.9 = (s32[8]{0:T(128)S(1)}, s32[8]{0:T(128)S(1)}, u32[]{:S(2)}, u32[]{:S(2)}) collective-permute-start(s32[8]{0:T(128)S(1)} %bitcast_add_fusion.label_ref), channel_id=1, source_target_pairs={{0,16},{16,0},{32,48},{48,32},{64,80},{80,64},{96,112},{112,96},{1... | collective-permute-start | bytes 104 | tf_op jit(solution)/shard_map/ppermute | solution.py:366
  42.2 14.9 %collective-permute-start.10 = (bf16[8,2,64,128]{3,2,1,0:T(8,128)(2,1)S(1)}, bf16[8,2,64,128]{3,2,1,0:T(8,128)(2,1)}, u32[]{:S(2)}, u32[]{:S(2)}) collective-permute-start(bf16[8,2,64,128]{3,2,1,0:T(8,128)(2,1)S(1)} %get-tuple-element.12.spec_hbm), channel_id=1, source_target_pairs={{0,16},{16,0},{32,48},{48,32},{64,80},{80,64},{96,112},{112,96},{1... | collective-permute-start | bytes 786440 | tf_op jit(solution)/shard_map/ppermute | solution.py:366
  43.2 13.9 %all-to-all-start.1 = ((f32[16,8,128]{2,1,0:T(8,128)}), f32[16,8,128]{2,1,0:T(8,128)S(1)}, u32[]{:S(2)}, u32[]{:S(2)}) async-start(f32[16,8,128]{2,1,0:T(8,128)} %broadcast_in_dim.5), calls=%async_computation.1 | async-start | bytes 131072 | tf_op jit(solution)/shard_map/all_to_all | solution.py:372
  57.1 1.0 %copy-start.10 = (bf16[256,512]{1,0:T(8,128)(2,1)S(1)}, bf16[256,512]{1,0:T(8,128)(2,1)}, u32[]{:S(2)}) copy-start(bf16[256,512]{1,0:T(8,128)(2,1)} %constant.85.pair_hbm) | copy-start | bytes 786436
  64.1 9.2 %copy-start.2 = (bf16[128,512]{1,0:T(8,128)(2,1)S(1)}, bf16[128,512]{1,0:T(8,128)(2,1)}, u32[]{:S(2)}) copy-start(bf16[128,512]{1,0:T(8,128)(2,1)} %constant.87.resist_t_hbm) | copy-start | bytes 393220
  64.1 9.2 %copy-start.3 = (bf16[512,128]{1,0:T(8,128)(2,1)S(1)}, bf16[512,128]{1,0:T(8,128)(2,1)}, u32[]{:S(2)}) copy-start(bf16[512,128]{1,0:T(8,128)(2,1)} %constant.86.resist_hbm) | copy-start | bytes 393220
  64.1 9.1 %collective-permute-start.11 = (bf16[8,128,128]{2,1,0:T(8,128)(2,1)S(1)}, bf16[8,128,128]{2,1,0:T(8,128)(2,1)S(1)}, u32[]{:S(2)}, u32[]{:S(2)}) collective-permute-start(bf16[8,128,128]{2,1,0:T(8,128)(2,1)S(1)} %image.3), channel_id=1, source_target_pairs={{0,16},{16,0},{32,48},{48,32},{64,80},{80,64},{96,112},{112,96},{1... | collective-permute-start | bytes 786440 | tf_op jit(solution)/shard_map/ppermute | solution.py:366

commit v2 on v1

--- a/solution.py
+++ b/solution.py
@@ -1,3 +1,5 @@
+import functools
+
 import jax
 import jax.numpy as jnp
 import numpy as np
@@ -44,12 +46,9 @@
     )
 
 
-def pair_table():
+def image_table():
     c, s = spectral_table(NF, Q)
-    z = np.zeros((NF, 2 * Q))
-    up = np.concatenate([c, s], axis=1)
-    down = np.concatenate([-s, c], axis=1)
-    return np.block([[up, z], [z, up], [down, z], [z, down]])
+    return np.concatenate([np.concatenate([c, s], axis=1), np.concatenate([-s, c], axis=1)], axis=0)
 
 
 def resist_table(pixels, samples):
@@ -82,20 +81,16 @@
 SMEM = pl.BlockSpec(memory_space=pltpu.SMEM)
 VMEM = pl.BlockSpec(memory_space=pltpu.VMEM)
 ANY = pl.BlockSpec(memory_space=pl.ANY)
-
-
-def analyse_kernel(
-    cell_ref, mask_hbm, wave_t_hbm, wave_hbm, row_hbm, col_hbm, spec_ref, height_ref,
-    mask, wave_t_ref, wave_ref, row_ref, col_ref, rows, along, sems, table_sems,
-):
+HBM = pl.BlockSpec(memory_space=pltpu.HBM)
+
+
+def density_kernel(cell_ref, mask_hbm, row_hbm, col_hbm, height_ref, mask, row_ref, col_ref, rows, along, sems, table_sems):
     def copy(t):
         return pltpu.make_async_copy(mask_hbm.at[t], mask.at[t], sems.at[t])
 
     tables = [
-        pltpu.make_async_copy(source, target, table_sems.at[at])
-        for at, (source, target) in enumerate(
-            ((row_hbm, row_ref), (col_hbm, col_ref), (wave_t_hbm, wave_t_ref), (wave_hbm, wave_ref))
-        )
+        pltpu.make_async_copy(row_hbm, row_ref, table_sems.at[0]),
+        pltpu.make_async_copy(col_hbm, col_ref, table_sems.at[1]),
     ]
     for t in range(2):
         copy(t).start()
@@ -103,11 +98,9 @@
         table.start()
     for t in range(2, TILES):
         copy(t).start()
+    left = lax.broadcasted_iota(jnp.int32, (B, 2 * BLK_PX), 1) < BLK_PX
     for table in tables:
         table.wait()
-    lower = lax.broadcasted_iota(jnp.int32, (NF, 2 * NF), 1) < NF
-    left = lax.broadcasted_iota(jnp.int32, (B, 2 * BLK_PX), 1) < BLK_PX
-    scale = 1.0 / P_SIZE
 
     def some_tiles(trip, carry):
         batch = [trip * 2, trip * 2 + 1]
@@ -127,14 +120,6 @@
                 spread = spread + first * col[2 * pair : 2 * pair + 1] + second * col[2 * pair + 1 : 2 * pair + 2]
             along[at, :] = spread
             rows[at, :] = row_ref[cell // SC]
-        for t in batch:
-            projected = jnp.dot(mask[t], wave_t_ref[...], preferred_element_type=F32).astype(BF16)
-            raw = jnp.dot(wave_ref[...], projected, preferred_element_type=F32)
-            turned = pltpu.roll(raw, NF, 1)
-            re = (raw[:NF] - turned[NF:]) * scale
-            im = (turned[:NF] + raw[NF:]) * (-scale)
-            spec_ref[t, 0] = jnp.where(lower, re, pltpu.roll(re, NF, 1)).astype(BF16)
-            spec_ref[t, 1] = jnp.where(lower, im, pltpu.roll(im, NF, 1)).astype(BF16)
         return carry
 
     lax.fori_loop(0, TILES // 2, some_tiles, 0)
@@ -148,43 +133,92 @@
     height_ref[...] = part
 
 
-def analyse(mask_tiles, cell_of_tile):
-    wave = wave_table()
+def density_heights(mask_tiles, cell_of_tile):
     row_part, col_part = height_tables()
     return pl.pallas_call(
-        analyse_kernel,
-        in_specs=[SMEM] + [ANY] * 5,
-        out_specs=[VMEM, VMEM],
-        out_shape=[
-            jax.ShapeDtypeStruct((TILES, 2, NF, 2 * NF), BF16),
-            jax.ShapeDtypeStruct((B, 4 * SC), F32),
-        ],
+        density_kernel,
+        in_specs=[SMEM] + [HBM] * 3,
+        out_specs=VMEM,
+        out_shape=jax.ShapeDtypeStruct((B, 4 * SC), F32),
         scratch_shapes=[
             pltpu.VMEM((TILES, P_SIZE, P_SIZE), BF16),
-            pltpu.VMEM((P_SIZE, 2 * NF), BF16),
-            pltpu.VMEM((2 * NF, P_SIZE), BF16),
             pltpu.VMEM((SC, B, 4 * SC), F32),
             pltpu.VMEM((SC, B, 4 * SC), F32),
             pltpu.VMEM((TILES * B, 4 * SC), F32),
             pltpu.VMEM((TILES * B, 4 * SC), F32),
             pltpu.SemaphoreType.DMA((TILES,)),
-            pltpu.SemaphoreType.DMA((4,)),
+            pltpu.SemaphoreType.DMA((2,)),
         ],
-        name="analyse",
-        compiler_params=pltpu.CompilerParams(vmem_limit_bytes=12 << 20),
-        cost_estimate=pl.CostEstimate(flops=10**9, bytes_accessed=6 * 10**6, transcendentals=0),
-    )(cell_of_tile, mask_tiles, as_bf16(wave.T), as_bf16(wave), jnp.asarray(row_part), jnp.asarray(col_part))
+        name="density",
+        cost_estimate=pl.CostEstimate(flops=10**7, bytes_accessed=5 * 10**6, transcendentals=0),
+    )(cell_of_tile, mask_tiles, jnp.asarray(row_part), jnp.asarray(col_part))
+
+
+def spectra_kernel(step, mask_hbm, wave_t_hbm, wave_hbm, spec_ref, mask, wave_t_ref, wave_ref, sems, table_sems):
+    def copy(t):
+        return pltpu.make_async_copy(mask_hbm.at[t], mask.at[t], sems.at[t])
+
+    tables = [
+        pltpu.make_async_copy(wave_t_hbm, wave_t_ref, table_sems.at[0]),
+        pltpu.make_async_copy(wave_hbm, wave_ref, table_sems.at[1]),
+    ]
+    for table in tables:
+        table.start()
+    for t in range(TILES):
+        copy(t).start()
+    lower = lax.broadcasted_iota(jnp.int32, (NF, 2 * NF), 1) < NF
+    scale = 1.0 / P_SIZE
+    for table in tables:
+        table.wait()
+
+    def some_tiles(trip, carry):
+        batch = [trip * step + at for at in range(step)]
+        for t in batch:
+            copy(t).wait()
+        every = mask[pl.ds(trip * step, step)].reshape(step * P_SIZE, P_SIZE)
+        projected = jnp.dot(every, wave_t_ref[...], preferred_element_type=F32).astype(BF16)
+        for at, t in enumerate(batch):
+            raw = jnp.dot(
+                wave_ref[...], projected[at * P_SIZE : (at + 1) * P_SIZE], preferred_element_type=F32
+            )
+            turned = pltpu.roll(raw, NF, 1)
+            re = (raw[:NF] - turned[NF:]) * scale
+            im = (turned[:NF] + raw[NF:]) * (-scale)
+            spec_ref[t, 0] = jnp.where(lower, re, pltpu.roll(re, NF, 1)).astype(BF16)
+            spec_ref[t, 1] = jnp.where(lower, im, pltpu.roll(im, NF, 1)).astype(BF16)
+        return carry
+
+    lax.fori_loop(0, TILES // step, some_tiles, 0)
+
+
+def form_spectra(mask_tiles, step=4):
+    wave = wave_table()
+    return pl.pallas_call(
+        functools.partial(spectra_kernel, step),
+        in_specs=[HBM] * 3,
+        out_specs=VMEM,
+        out_shape=jax.ShapeDtypeStruct((TILES, 2, NF, 2 * NF), BF16),
+        scratch_shapes=[
+            pltpu.VMEM((TILES, P_SIZE, P_SIZE), BF16),
+            pltpu.VMEM((P_SIZE, 2 * NF), BF16),
+            pltpu.VMEM((2 * NF, P_SIZE), BF16),
+            pltpu.SemaphoreType.DMA((TILES,)),
+            pltpu.SemaphoreType.DMA((2,)),
+        ],
+        name="spectra",
+        cost_estimate=pl.CostEstimate(flops=10**9, bytes_accessed=5 * 10**6, transcendentals=0),
+    )(mask_tiles, as_bf16(wave.T), as_bf16(wave))
 
 
 def image_kernel(
     first_ref, second_ref, first_div_ref, second_div_ref, label_ref, centre_ref, height_ref,
-    spec_hbm, left_hbm, pair_hbm, *rest
+    spec_hbm, left_hbm, right_hbm, *rest
 ):
-    pieces, (out_ref, held, spec_ref, left_ref, pair_ref, sems, table_sems) = rest[:8], rest[8:]
+    pieces, (out_ref, held, spec_ref, left_ref, right_ref, pair_ref, sems, table_sems) = rest[:8], rest[8:]
     tables = [
         pltpu.make_async_copy(source, target, table_sems.at[at])
         for at, (source, target) in enumerate(
-            ((spec_hbm, spec_ref), (left_hbm, left_ref), (pair_hbm, pair_ref))
+            ((right_hbm, right_ref), (left_hbm, left_ref), (spec_hbm, spec_ref))
         )
     ]
     for table in tables:
@@ -211,6 +245,11 @@
 
     for table in tables:
         table.wait()
+    for at in range(4):
+        rows = slice(at * NF, (at + 1) * NF)
+        block = right_ref[(at // 2) * NF : (at // 2 + 1) * NF]
+        pair_ref[rows, (at % 2) * 2 * Q : (at % 2 + 1) * 2 * Q] = block
+        pair_ref[rows, (1 - at % 2) * 2 * Q : (2 - at % 2) * 2 * Q] = jnp.zeros_like(block)
 
     def some_tiles(trip, carry):
         batch = [trip * 4 + at for at in range(4)]
@@ -259,13 +298,14 @@
 def image(place, labels, centre, heights, spectra, pieces):
     return pl.pallas_call(
         image_kernel,
-        in_specs=[SMEM] * 6 + [VMEM] + [ANY] * 11,
+        in_specs=[SMEM] * 6 + [VMEM, ANY, HBM, HBM] + [ANY] * 8,
         out_specs=VMEM,
         out_shape=jax.ShapeDtypeStruct((TILES, Q, Q), BF16),
         scratch_shapes=[
             pltpu.VMEM((TILES, GROUPS, 4, NF, 4 * NF), BF16),
             pltpu.VMEM((TILES, 2, NF, 2 * NF), BF16),
             pltpu.VMEM((2 * Q, 2 * NF), BF16),
+            pltpu.VMEM((2 * NF, 2 * Q), BF16),
             pltpu.VMEM((4 * NF, 4 * Q), BF16),
             pltpu.SemaphoreType.DMA((TILES,)),
             pltpu.SemaphoreType.DMA((3,)),
@@ -273,7 +313,7 @@
         name="image",
         compiler_params=pltpu.CompilerParams(vmem_limit_bytes=16 << 20),
         cost_estimate=pl.CostEstimate(flops=3 * 10**9, bytes_accessed=4 * 10**6, transcendentals=0),
-    )(*place, labels, centre, heights, spectra, as_bf16(left_table()), as_bf16(pair_table()), *pieces)
+    )(*place, labels, centre, heights, spectra, as_bf16(left_table()), as_bf16(image_table()), *pieces)
 
 
 def resist_kernel(
@@ -320,7 +360,7 @@
     table = resist_table(P_SIZE, Q)
     return pl.pallas_call(
         resist_kernel,
-        in_specs=[ANY] * 4,
+        in_specs=[ANY, ANY, HBM, HBM],
         out_specs=ANY,
         out_shape=jax.ShapeDtypeStruct((TILES, P_SIZE, P_SIZE), BF16),
         scratch_shapes=[
@@ -393,7 +433,7 @@
     before = send(mine, 0, 1)
     after = send(mine, 0, -1)
     far = send(mine, 0, 2)
-    spectra, heights = analyse(mask_tiles, cell_of_tile)
+    heights = density_heights(mask_tiles, cell_of_tile)
     low = jnp.stack([mine, after_all(before, heights)])
     high = jnp.stack([after_all(far, heights), after])
     low_before = send(low, 1, 1)
@@ -401,6 +441,7 @@
     high_before = send(high, 1, 1)
     low_after = send(low, 1, -1)
     heights = summed(heights, "tile")
+    spectra = form_spectra(mask_tiles)
     low_far = send(after_all(low_before, heights), 1, 1)
     high_far = send(after_all(high_after, heights), 1, -1)
     heights = summed(heights, "focus")

time: 77.3 us -> 77.2 us (level)
  Pallas kernels: 22.2 us -> 25.4 us
  local copies, waits for them, and re-layouts: 7.98 us -> 4.82 us
  waiting for transfers between devices: 11.2 us -> 9.06 us
  starting transfers between devices: 22 us -> 23.4 us
  other arithmetic: 1.3 us -> 2.13 us
    all_to_all x1, waiting for transfers between devices: 10.3 us -> 7.03 us  [summed(): return jnp.sum(lax.all_to_all(copies, axis, 0, 0, tiled=True), axis=0)]
    pallas_call x4 -> x5, Pallas kernels: 22.2 us -> 25.4 us  [the longest x2 12.2 us: image(): pl.pallas_call(image_kernel, in_specs=[SMEM] * 6 + [VMEM, ANY, HBM, HBM]...]
    unnamed x26 -> x20, local copies, waits for them, and re-layouts: 4.25 us -> 1.19 us
    ppermute x9, waiting for transfers between devices: 0.02 us -> 2.03 us  [send(): return lax.ppermute(value, ALL, ring(phase, step))]
    ppermute x9, starting transfers between devices: 13.3 us -> 14.5 us  [send(): return lax.ppermute(value, ALL, ring(phase, step))]
    all_to_all x1, starting transfers between devices: 3.5 us -> 4.55 us  [summed(): return jnp.sum(lax.all_to_all(copies, axis, 0, 0, tiled=True), axis=0)]
    ppermute x3, starting transfers between devices: 5.21 us -> 4.32 us  [partner(): return lax.ppermute(x, 'tile', [(t, t ^ 1) for t in range(8)])]
    reduce_sum x2, other arithmetic: 0.03 us -> 0.87 us  [summed(): return jnp.sum(lax.all_to_all(copies, axis, 0, 0, tiled=True), axis=0)]
  transfers between devices with their start and end apart: 13 -> 13, of which waited for: 2 -> 2; matrix products, arithmetic and copies ran while one was open for 3% -> 5% of each run, Pallas kernels for 16% -> 20%
where the time goes in v2:
time: 77.2 us; the launch traced here: 76.8 us
  Pallas kernels  25.4 us (33%)
  starting transfers between devices  23.4 us (30%)
  blocking collectives  11.7 us (15%)
  waiting for transfers between devices  9.06 us (12%)
  local copies, waits for them, and re-layouts  4.82 us (6%)
  other arithmetic  2.13 us (3%)
    ppermute x9, starting transfers between devices, send(): return lax.ppermute(value, ALL, ring(phase, step))  14.5 us
    pallas_call x2, Pallas kernels, image(): pl.pallas_call(image_kernel, in_specs=[SMEM] * 6 + [VMEM, ANY, HBM, HBM]...  12.2 us
    all_to_all x1, blocking collectives, summed(): return jnp.sum(lax.all_to_all(copies, axis, 0, 0, tiled=True), axis=0)  11.7 us
    all_to_all x1, waiting for transfers between devices, summed(): return jnp.sum(lax.all_to_all(copies, axis, 0, 0, tiled=True), axis=0)  7.03 us
    pallas_call x1, Pallas kernels, form_spectra(): pl.pallas_call(functools.partial(spectra_kernel, step), in_specs=[HBM] *...  5.15 us
    all_to_all x1, starting transfers between devices, summed(): return jnp.sum(lax.all_to_all(copies, axis, 0, 0, tiled=True), axis=0)  4.55 us
    pallas_call x1, Pallas kernels, density_heights(): pl.pallas_call(density_kernel, in_specs=[SMEM] + [HBM] * 3, out_specs=VME...  4.45 us
    ppermute x3, starting transfers between devices, partner(): return lax.ppermute(x, 'tile', [(t, t ^ 1) for t in range(8)])  4.32 us
  transfers between devices with their start and end apart: 13, of which 2 were waited for; matrix products, arithmetic and copies ran while one was open for 5% of the time, Pallas kernels for 20%

profile of v2, /device:TPU:1, one launch (start us, length us, event | category | flops | bytes accessed | tf_op | source)
XLA Modules:
  0.0 76.8 jit_solution(17680273638213174274)
XLA Ops:
  0.0 1.1 %copy-done = bf16[1,24,4,4096]{3,2,1,0:T(4,128)(2,1)S(1)} copy-done((bf16[1,24,4,4096]{3,2,1,0:T(4,128)(2,1)S(1)}, bf16[1,24,4,4096]{3,2,1,0:T(4,128)(2,1)}, u32[]{:S(2)}) %copy-start) | copy-done | bytes 786456
  1.1 0.2 constant_dynamic-slice_fusion
  1.3 0.6 reshape.28
  1.9 0.6 copy.18
  2.5 0.5 reshape.29
  3.0 0.0 copy-start.8
  3.0 0.0 copy-start.9
  3.0 3.6 %collective-permute-start.1 = (bf16[3,4,64,256]{3,2,1,0:T(8,128)(2,1)S(1)}, bf16[3,4,64,256]{3,2,1,0:T(8,128)(2,1)S(1)}, u32[]{:S(2)}, u32[]{:S(2)}) collective-permute-start(bf16[3,4,64,256]{3,2,1,0:T(8,128)(2,1)S(1)} %reshape.29), channel_id=1, source_target_pairs={{0,2},{1,3},{2,0},{3,1},{4,6},{5,7},{6,4},{7,5},{8,10},{9,11},{10,... | collective-permute-start | bytes 1179656 | tf_op jit(solution)/shard_map/ppermute | solution.py:398
  6.7 0.3 collective-permute-start
  7.0 2.4 %collective-permute-start.2 = (bf16[3,4,64,256]{3,2,1,0:T(8,128)(2,1)S(1)}, bf16[3,4,64,256]{3,2,1,0:T(8,128)(2,1)}, u32[]{:S(2)}, u32[]{:S(2)}) collective-permute-start(bf16[3,4,64,256]{3,2,1,0:T(8,128)(2,1)S(1)} %reshape.29), channel_id=1, source_target_pairs={{0,3},{1,0},{2,1},{3,2},{4,7},{5,4},{6,5},{7,6},{8,11},{9,8},{10,9... | collective-permute-start | bytes 1179656 | tf_op jit(solution)/shard_map/ppermute | solution.py:398
  9.4 0.5 stack_reshape.3
  9.8 4.4 %density.1 = f32[8,128]{1,0:T(8,128)} custom-call(s32[8]{0:T(128)} %cell_ref.1, bf16[8,512,512]{2,1,0:T(8,128)(2,1)} %mask_hbm.3, f32[32,8,128]{2,1,0:T(8,128)} %constant.70.clone.row_hbm, f32[32,8,128]{2,1,0:T(8,128)} %constant.71.clone.col_hbm), custom_call_target="tpu_custom_call" | custom-call | flops 10000000 | bytes 5000000 | tf_op jit(solution)/shard_map/density/pallas_call | solution.py:138
  14.3 0.0 copy-start.4
  14.3 0.0 copy-start.5
  14.3 0.0 copy-start.6
  14.3 0.0 collective-permute-done.1
  14.3 0.0 copy-start.7
  14.3 2.0 %collective-permute-done = bf16[3,4,64,256]{3,2,1,0:T(8,128)(2,1)S(1)} collective-permute-done((bf16[3,4,64,256]{3,2,1,0:T(8,128)(2,1)S(1)}, bf16[3,4,64,256]{3,2,1,0:T(8,128)(2,1)S(1)}, u32[]{:S(2)}, u32[]{:S(2)}) %collective-permute-start) | collective-permute-done | bytes 393248 | tf_op jit(solution)/shard_map/ppermute | solution.py:398
  16.4 0.1 pad_maximum_fusion.rest_0_
  16.4 1.3 %collective-permute-start.3 = (bf16[2,3,4,64,256]{4,3,2,1,0:T(8,128)(2,1)S(1)}, bf16[2,3,4,64,256]{4,3,2,1,0:T(8,128)(2,1)S(1)}, u32[]{:S(2)}, u32[]{:S(2)}) collective-permute-start(bf16[2,3,4,64,256]{4,3,2,1,0:T(8,128)(2,1)S(1)} %pad_maximum_fusion.rest_0_), channel_id=1, source_target_pairs={{0,4},{1,5},{2,6},{3,7},{4,8},{5,9},{6,10},{7,11},{8,12},{9,13},{1... | collective-permute-start | bytes 2359304 | tf_op jit(solution)/shard_map/ppermute | solution.py:398
  17.7 1.2 %pad_maximum_fusion.1.rest_1_ = bf16[2,3,4,64,256]{4,3,2,1,0:T(8,128)(2,1)S(1)} fusion(bf16[1,3,4,64,256]{4,3,2,1,0:T(8,128)(2,1)} %bitcast.8, bf16[1,3,4,64,256]{4,3,2,1,0:T(8,128)(2,1)} %bitcast.11), kind=kLoop, calls=%fused_computation.1 | loop fusion | flops 393216 | bytes 1572864 | tf_op jit(solution)/shard_map/stack | solution.py:438
  18.9 1.9 %collective-permute-start.6 = (bf16[2,3,4,64,256]{4,3,2,1,0:T(8,128)(2,1)S(1)}, bf16[2,3,4,64,256]{4,3,2,1,0:T(8,128)(2,1)}, u32[]{:S(2)}, u32[]{:S(2)}) collective-permute-start(bf16[2,3,4,64,256]{4,3,2,1,0:T(8,128)(2,1)S(1)} %pad_maximum_fusion.1.rest_1_), channel_id=1, source_target_pairs={{0,12},{1,13},{2,14},{3,15},{4,0},{5,1},{6,2},{7,3},{8,4},{9,5},{1... | collective-permute-start | bytes 2359304 | tf_op jit(solution)/shard_map/ppermute | solution.py:398
  20.9 0.7 broadcast_in_dim.4
  21.5 11.7 %all_to_all.10 = f32[8,8,128]{2,1,0:T(8,128)S(1)} all-to-all(f32[8,8,128]{2,1,0:T(8,128)S(1)} %broadcast_in_dim.4), channel_id=1, replica_groups=mesh['tile'=8,'focus'=16] {'tile'}, dimensions={0} | all-to-all | bytes 65536 | tf_op jit(solution)/shard_map/all_to_all | solution.py:412
  33.3 2.2 %collective-permute-start.8 = (bf16[2,3,4,64,256]{4,3,2,1,0:T(8,128)(2,1)S(1)}, bf16[2,3,4,64,256]{4,3,2,1,0:T(8,128)(2,1)}, u32[]{:S(2)}, u32[]{:S(2)}) collective-permute-start(bf16[2,3,4,64,256]{4,3,2,1,0:T(8,128)(2,1)S(1)} %pad_maximum_fusion.rest_0_), channel_id=1, source_target_pairs={{0,12},{1,13},{2,14},{3,15},{4,0},{5,1},{6,2},{7,3},{8,4},{9,5},{1... | collective-permute-start | bytes 2359304 | tf_op jit(solution)/shard_map/ppermute | solution.py:398
  35.5 0.0 collective-permute-start.4
  35.5 0.0 collective-permute-done.3.rest_2_
  35.5 0.8 collective-permute-start.5
  36.2 0.0 collective-permute-done.6.rest_7_
  36.2 2.0 %collective-permute-start.7 = (bf16[2,3,4,64,256]{4,3,2,1,0:T(8,128)(2,1)}, bf16[2,3,4,64,256]{4,3,2,1,0:T(8,128)(2,1)}, u32[]{:S(2)}, u32[]{:S(2)}) collective-permute-start(bf16[2,3,4,64,256]{4,3,2,1,0:T(8,128)(2,1)} %collective-permute-done.6.rest_7_), channel_id=1, source_target_pairs={{0,12},{1,13},{2,14},{3,15},{4,0},{5,1},{6,2},{7,3},{8,4},{9,5},{1... | collective-permute-start | bytes 2359304 | tf_op jit(solution)/shard_map/ppermute | solution.py:398
  38.2 1.1 %collective-permute-start.9 = (s32[8]{0:T(128)S(1)}, s32[8]{0:T(128)S(1)}, u32[]{:S(2)}, u32[]{:S(2)}) collective-permute-start(s32[8]{0:T(128)S(1)} %bitcast_add_fusion.label_ref), channel_id=1, source_target_pairs={{0,16},{16,0},{32,48},{48,32},{64,80},{80,64},{96,112},{112,96},{1... | collective-permute-start | bytes 104 | tf_op jit(solution)/shard_map/ppermute | solution.py:406
  39.4 5.2 %spectra.1.spec_hbm = bf16[8,2,64,128]{3,2,1,0:T(8,128)(2,1)} custom-call(bf16[8,512,512]{2,1,0:T(8,128)(2,1)} %mask_hbm.3, bf16[512,128]{1,0:T(8,128)(2,1)} %constant.82.wave_t_hbm, bf16[128,512]{1,0:T(8,128)(2,1)} %constant.83.wave_hbm), custom_call_target="tpu_custom_call" | custom-call | flops 1000000000 | bytes 5000000 | tf_op jit(solution)/shard_map/spectra/pallas_call | solution.py:196
  44.5 0.0 collective-permute-done.9.label_ref
  44.5 0.1 collective-permute-start.10
  44.6 0.6 broadcast_in_dim.5
  45.3 4.5 %all-to-all-start.1 = ((f32[16,8,128]{2,1,0:T(8,128)}), f32[16,8,128]{2,1,0:T(8,128)}, u32[]{:S(2)}, u32[]{:S(2)}) async-start(f32[16,8,128]{2,1,0:T(8,128)} %broadcast_in_dim.5), calls=%async_computation.1 | async-start | bytes 131072 | tf_op jit(solution)/shard_map/all_to_all | solution.py:412
  49.8 7.0 %all-to-all-done.1 = f32[16,8,128]{2,1,0:T(8,128)} async-done(((f32[16,8,128]{2,1,0:T(8,128)}), f32[16,8,128]{2,1,0:T(8,128)}, u32[]{:S(2)}, u32[]{:S(2)}) %all-to-all-start.1) | async-done | bytes 65568 | tf_op jit(solution)/shard_map/all_to_all | solution.py:412
  56.9 0.9 %reduce_sum.19.height_ref = f32[8,128]{1,0:T(8,128)S(1)} reduce(f32[16,8,128]{2,1,0:T(8,128)} %all-to-all-done.1, f32[]{:T(128)} %constant.67.clone.1), dimensions={0}, to_apply=%region_1.2 | reduce | flops 15360 | bytes 69636 | tf_op jit(solution)/shard_map/reduce_sum | solution.py:412
  57.7 0.0 collective-permute-done.8.rest_6_
  57.8 0.0 collective-permute-done.5.rest_4_
  57.8 0.0 collective-permute-done.7.rest_5_
  57.8 0.0 copy-start.1
  57.8 6.0 %image.3 = bf16[8,128,128]{2,1,0:T(8,128)(2,1)S(1)} custom-call(s32[1]{0:T(128)} %bitcast.first_ref, s32[1]{0:T(128)} %bitcast.1.second_ref, s32[1]{0:T(128)} %bitcast.2.first_div_ref, s32[1]{0:T(128)} %bitcast.3.second_div_ref, s32[8]{0:T(128)S(1)} %collective-permute-done.9.label_ref, f32[16]{0:T(128)S(1)} %copy-done.4, ...), custom_call_target="tpu_custom_call" | custom-call | flops 3000000000 | bytes 4000000 | tf_op jit(solution)/shard_map/image/pallas_call | solution.py:299
  63.9 0.0 copy-start.2
  63.9 0.0 copy-start.3
  63.9 3.1 %collective-permute-start.11 = (bf16[8,128,128]{2,1,0:T(8,128)(2,1)S(1)}, bf16[8,128,128]{2,1,0:T(8,128)(2,1)S(1)}, u32[]{:S(2)}, u32[]{:S(2)}) collective-permute-start(bf16[8,128,128]{2,1,0:T(8,128)(2,1)S(1)} %image.3), channel_id=1, source_target_pairs={{0,16},{16,0},{32,48},{48,32},{64,80},{80,64},{96,112},{112,96},{1... | collective-permute-start | bytes 786440 | tf_op jit(solution)/shard_map/ppermute | solution.py:406
  67.0 6.1 %image.2.own_hbm = bf16[8,128,128]{2,1,0:T(8,128)(2,1)S(1)} custom-call(s32[1]{0:T(128)} %bitcast.first_ref, s32[1]{0:T(128)} %bitcast.1.second_ref, s32[1]{0:T(128)} %bitcast.2.first_div_ref, s32[1]{0:T(128)} %bitcast.3.second_div_ref, s32[8]{0:T(128)S(1)} %bitcast_add_fusion.label_ref, f32[16]{0:T(128)S(1)} %copy-done.4, ...), custom_call_target="tpu_custom_call" | custom-call | flops 3000000000 | bytes 4000000 | tf_op jit(solution)/shard_map/image/pallas_call | solution.py:299
  73.2 3.6 %resist.1 = bf16[8,512,512]{2,1,0:T(8,128)(2,1)} custom-call(bf16[8,128,128]{2,1,0:T(8,128)(2,1)S(1)} %image.2.own_hbm, bf16[8,128,128]{2,1,0:T(8,128)(2,1)S(1)} %collective-permute-done.11.other_hbm, bf16[512,128]{1,0:T(8,128)(2,1)S(1)} %copy-done.3, bf16[128,512]{1,0:T(8,128)(2,1)S(1)} %copy-done.2), custom_call_target="tpu_custom_call" | custom-call | flops 1000000000 | bytes 5000000 | tf_op jit(solution)/shard_map/resist/pallas_call | solution.py:361
  (16 shorter events, 0.0 us)
Async XLA Ops:
  0.0 1.1 %copy-start = (bf16[1,24,4,4096]{3,2,1,0:T(4,128)(2,1)S(1)}, bf16[1,24,4,4096]{3,2,1,0:T(4,128)(2,1)}, u32[]{:S(2)}) copy-start(bf16[1,24,4,4096]{3,2,1,0:T(4,128)(2,1)} %param.18) | copy-start | bytes 2359300
  3.0 35.2 %copy-start.8 = (s32[8]{0:T(128)S(1)}, s32[8]{0:T(128)}, u32[]{:S(2)}) copy-start(s32[8]{0:T(128)} %cell_ref.1) | copy-start | bytes 100
  3.0 35.2 %copy-start.9 = (s32[8,1]{0,1:T(1,128)S(1)}, s32[8,1]{0,1:T(1,128)}, u32[]{:S(2)}) copy-start(s32[8,1]{0,1:T(1,128)} %param.16) | copy-start | bytes 100
  3.0 11.3 %collective-permute-start.1 = (bf16[3,4,64,256]{3,2,1,0:T(8,128)(2,1)S(1)}, bf16[3,4,64,256]{3,2,1,0:T(8,128)(2,1)S(1)}, u32[]{:S(2)}, u32[]{:S(2)}) collective-permute-start(bf16[3,4,64,256]{3,2,1,0:T(8,128)(2,1)S(1)} %reshape.29), channel_id=1, source_target_pairs={{0,2},{1,3},{2,0},{3,1},{4,6},{5,7},{6,4},{7,5},{8,10},{9,11},{10,... | collective-permute-start | bytes 1179656 | tf_op jit(solution)/shard_map/ppermute | solution.py:398
  6.7 9.7 %collective-permute-start = (bf16[3,4,64,256]{3,2,1,0:T(8,128)(2,1)S(1)}, bf16[3,4,64,256]{3,2,1,0:T(8,128)(2,1)S(1)}, u32[]{:S(2)}, u32[]{:S(2)}) collective-permute-start(bf16[3,4,64,256]{3,2,1,0:T(8,128)(2,1)S(1)} %reshape.29), channel_id=1, source_target_pairs={{0,1},{1,2},{2,3},{3,0},{4,5},{5,6},{6,7},{7,4},{8,9},{9,10},{10,1... | collective-permute-start | bytes 1179656 | tf_op jit(solution)/shard_map/ppermute | solution.py:398
  7.0 10.7 %collective-permute-start.2 = (bf16[3,4,64,256]{3,2,1,0:T(8,128)(2,1)S(1)}, bf16[3,4,64,256]{3,2,1,0:T(8,128)(2,1)}, u32[]{:S(2)}, u32[]{:S(2)}) collective-permute-start(bf16[3,4,64,256]{3,2,1,0:T(8,128)(2,1)S(1)} %reshape.29), channel_id=1, source_target_pairs={{0,3},{1,0},{2,1},{3,2},{4,7},{5,4},{6,5},{7,6},{8,11},{9,8},{10,9... | collective-permute-start | bytes 1179656 | tf_op jit(solution)/shard_map/ppermute | solution.py:398
  14.3 43.5 %copy-start.4 = (f32[16]{0:T(128)S(1)}, f32[16]{0:T(128)}, u32[]{:S(2)}) copy-start(f32[16]{0:T(128)} %centre_ref.3) | copy-start | bytes 196
  14.3 43.5 %copy-start.5 = (bf16[128,256]{1,0:T(8,128)(2,1)S(1)}, bf16[128,256]{1,0:T(8,128)(2,1)}, u32[]{:S(2)}) copy-start(bf16[128,256]{1,0:T(8,128)(2,1)} %constant.85.right_hbm) | copy-start | bytes 196612
  14.3 43.5 %copy-start.6 = (bf16[256,128]{1,0:T(8,128)(2,1)S(1)}, bf16[256,128]{1,0:T(8,128)(2,1)}, u32[]{:S(2)}) copy-start(bf16[256,128]{1,0:T(8,128)(2,1)} %constant.84.left_hbm) | copy-start | bytes 196612
  14.3 3.4 %copy-start.7 = (bf16[3,4,64,256]{3,2,1,0:T(8,128)(2,1)}, bf16[3,4,64,256]{3,2,1,0:T(8,128)(2,1)S(1)}, u32[]{:S(2)}) copy-start(bf16[3,4,64,256]{3,2,1,0:T(8,128)(2,1)S(1)} %collective-permute-done.1) | copy-start | bytes 1179652
  16.4 19.0 %collective-permute-start.3 = (bf16[2,3,4,64,256]{4,3,2,1,0:T(8,128)(2,1)S(1)}, bf16[2,3,4,64,256]{4,3,2,1,0:T(8,128)(2,1)S(1)}, u32[]{:S(2)}, u32[]{:S(2)}) collective-permute-start(bf16[2,3,4,64,256]{4,3,2,1,0:T(8,128)(2,1)S(1)} %pad_maximum_fusion.rest_0_), channel_id=1, source_target_pairs={{0,4},{1,5},{2,6},{3,7},{4,8},{5,9},{6,10},{7,11},{8,12},{9,13},{1... | collective-permute-start | bytes 2359304 | tf_op jit(solution)/shard_map/ppermute | solution.py:398
  18.9 17.3 %collective-permute-start.6 = (bf16[2,3,4,64,256]{4,3,2,1,0:T(8,128)(2,1)S(1)}, bf16[2,3,4,64,256]{4,3,2,1,0:T(8,128)(2,1)}, u32[]{:S(2)}, u32[]{:S(2)}) collective-permute-start(bf16[2,3,4,64,256]{4,3,2,1,0:T(8,128)(2,1)S(1)} %pad_maximum_fusion.1.rest_1_), channel_id=1, source_target_pairs={{0,12},{1,13},{2,14},{3,15},{4,0},{5,1},{6,2},{7,3},{8,4},{9,5},{1... | collective-permute-start | bytes 2359304 | tf_op jit(solution)/shard_map/ppermute | solution.py:398
  33.3 24.5 %collective-permute-start.8 = (bf16[2,3,4,64,256]{4,3,2,1,0:T(8,128)(2,1)S(1)}, bf16[2,3,4,64,256]{4,3,2,1,0:T(8,128)(2,1)}, u32[]{:S(2)}, u32[]{:S(2)}) collective-permute-start(bf16[2,3,4,64,256]{4,3,2,1,0:T(8,128)(2,1)S(1)} %pad_maximum_fusion.rest_0_), channel_id=1, source_target_pairs={{0,12},{1,13},{2,14},{3,15},{4,0},{5,1},{6,2},{7,3},{8,4},{9,5},{1... | collective-permute-start | bytes 2359304 | tf_op jit(solution)/shard_map/ppermute | solution.py:398
  35.5 22.3 %collective-permute-start.4 = (bf16[2,3,4,64,256]{4,3,2,1,0:T(8,128)(2,1)S(1)}, bf16[2,3,4,64,256]{4,3,2,1,0:T(8,128)(2,1)}, u32[]{:S(2)}, u32[]{:S(2)}) collective-permute-start(bf16[2,3,4,64,256]{4,3,2,1,0:T(8,128)(2,1)S(1)} %pad_maximum_fusion.1.rest_1_), channel_id=1, source_target_pairs={{0,4},{1,5},{2,6},{3,7},{4,8},{5,9},{6,10},{7,11},{8,12},{9,13},{1... | collective-permute-start | bytes 2359304 | tf_op jit(solution)/shard_map/ppermute | solution.py:398
  35.5 22.3 %collective-permute-start.5 = (bf16[2,3,4,64,256]{4,3,2,1,0:T(8,128)(2,1)S(1)}, bf16[2,3,4,64,256]{4,3,2,1,0:T(8,128)(2,1)}, u32[]{:S(2)}, u32[]{:S(2)}) collective-permute-start(bf16[2,3,4,64,256]{4,3,2,1,0:T(8,128)(2,1)S(1)} %collective-permute-done.3.rest_2_), channel_id=1, source_target_pairs={{0,4},{1,5},{2,6},{3,7},{4,8},{5,9},{6,10},{7,11},{8,12},{9,13},{1... | collective-permute-start | bytes 2359304 | tf_op jit(solution)/shard_map/ppermute | solution.py:398
  36.2 21.5 %collective-permute-start.7 = (bf16[2,3,4,64,256]{4,3,2,1,0:T(8,128)(2,1)}, bf16[2,3,4,64,256]{4,3,2,1,0:T(8,128)(2,1)}, u32[]{:S(2)}, u32[]{:S(2)}) collective-permute-start(bf16[2,3,4,64,256]{4,3,2,1,0:T(8,128)(2,1)} %collective-permute-done.6.rest_7_), channel_id=1, source_target_pairs={{0,12},{1,13},{2,14},{3,15},{4,0},{5,1},{6,2},{7,3},{8,4},{9,5},{1... | collective-permute-start | bytes 2359304 | tf_op jit(solution)/shard_map/ppermute | solution.py:398
  38.2 6.3 %collective-permute-start.9 = (s32[8]{0:T(128)S(1)}, s32[8]{0:T(128)S(1)}, u32[]{:S(2)}, u32[]{:S(2)}) collective-permute-start(s32[8]{0:T(128)S(1)} %bitcast_add_fusion.label_ref), channel_id=1, source_target_pairs={{0,16},{16,0},{32,48},{48,32},{64,80},{80,64},{96,112},{112,96},{1... | collective-permute-start | bytes 104 | tf_op jit(solution)/shard_map/ppermute | solution.py:406
  44.5 13.2 %collective-permute-start.10 = (bf16[8,2,64,128]{3,2,1,0:T(8,128)(2,1)}, bf16[8,2,64,128]{3,2,1,0:T(8,128)(2,1)S(1)}, u32[]{:S(2)}, u32[]{:S(2)}) collective-permute-start(bf16[8,2,64,128]{3,2,1,0:T(8,128)(2,1)} %spectra.1.spec_hbm), channel_id=1, source_target_pairs={{0,16},{16,0},{32,48},{48,32},{64,80},{80,64},{96,112},{112,96},{1... | collective-permute-start | bytes 786440 | tf_op jit(solution)/shard_map/ppermute | solution.py:406
  45.3 11.6 %all-to-all-start.1 = ((f32[16,8,128]{2,1,0:T(8,128)}), f32[16,8,128]{2,1,0:T(8,128)}, u32[]{:S(2)}, u32[]{:S(2)}) async-start(f32[16,8,128]{2,1,0:T(8,128)} %broadcast_in_dim.5), calls=%async_computation.1 | async-start | bytes 131072 | tf_op jit(solution)/shard_map/all_to_all | solution.py:412
  57.8 9.2 %copy-start.1 = (bf16[8,2,64,128]{3,2,1,0:T(8,128)(2,1)S(1)}, bf16[8,2,64,128]{3,2,1,0:T(8,128)(2,1)}, u32[]{:S(2)}) copy-start(bf16[8,2,64,128]{3,2,1,0:T(8,128)(2,1)} %spectra.1.spec_hbm) | copy-start | bytes 786436
  63.9 9.3 %copy-start.2 = (bf16[128,512]{1,0:T(8,128)(2,1)S(1)}, bf16[128,512]{1,0:T(8,128)(2,1)}, u32[]{:S(2)}) copy-start(bf16[128,512]{1,0:T(8,128)(2,1)} %constant.87.resist_t_hbm) | copy-start | bytes 393220
  63.9 9.3 %copy-start.3 = (bf16[512,128]{1,0:T(8,128)(2,1)S(1)}, bf16[512,128]{1,0:T(8,128)(2,1)}, u32[]{:S(2)}) copy-start(bf16[512,128]{1,0:T(8,128)(2,1)} %constant.86.resist_hbm) | copy-start | bytes 393220
  63.9 9.3 %collective-permute-start.11 = (bf16[8,128,128]{2,1,0:T(8,128)(2,1)S(1)}, bf16[8,128,128]{2,1,0:T(8,128)(2,1)S(1)}, u32[]{:S(2)}, u32[]{:S(2)}) collective-permute-start(bf16[8,128,128]{2,1,0:T(8,128)(2,1)S(1)} %image.3), channel_id=1, source_target_pairs={{0,16},{16,0},{32,48},{48,32},{64,80},{80,64},{96,112},{112,96},{1... | collective-permute-start | bytes 786440 | tf_op jit(solution)/shard_map/ppermute | solution.py:406

commit v3 on v2

--- a/solution.py
+++ b/solution.py
@@ -37,13 +37,6 @@
 
 def wave_table():
     return np.concatenate(spectral_table(NF, P_SIZE), axis=0)
-
-
-def left_table():
-    c, s = spectral_table(NF, Q)
-    return np.concatenate(
-        [np.concatenate([c.T, -s.T], axis=1), np.concatenate([s.T, c.T], axis=1)], axis=0
-    )
 
 
 def image_table():
@@ -130,16 +123,16 @@
     part = jnp.zeros((B, 4 * SC), F32)
     for q in range(4):
         part = jnp.where(quarter == q, whole[q * B : (q + 1) * B], part)
-    height_ref[...] = part
-
-
-def density_heights(mask_tiles, cell_of_tile):
+    height_ref[...] = jnp.broadcast_to(part[None], height_ref.shape)
+
+
+def density_heights(mask_tiles, cell_of_tile, copies):
     row_part, col_part = height_tables()
     return pl.pallas_call(
         density_kernel,
         in_specs=[SMEM] + [HBM] * 3,
         out_specs=VMEM,
-        out_shape=jax.ShapeDtypeStruct((B, 4 * SC), F32),
+        out_shape=jax.ShapeDtypeStruct((copies, B, 4 * SC), F32),
         scratch_shapes=[
             pltpu.VMEM((TILES, P_SIZE, P_SIZE), BF16),
             pltpu.VMEM((SC, B, 4 * SC), F32),
@@ -212,13 +205,13 @@
 
 def image_kernel(
     first_ref, second_ref, first_div_ref, second_div_ref, label_ref, centre_ref, height_ref,
-    spec_hbm, left_hbm, right_hbm, *rest
+    spec_hbm, right_hbm, *rest
 ):
     pieces, (out_ref, held, spec_ref, left_ref, right_ref, pair_ref, sems, table_sems) = rest[:8], rest[8:]
     tables = [
         pltpu.make_async_copy(source, target, table_sems.at[at])
         for at, (source, target) in enumerate(
-            ((right_hbm, right_ref), (left_hbm, left_ref), (spec_hbm, spec_ref))
+            ((right_hbm, right_ref), (spec_hbm, spec_ref))
         )
     ]
     for table in tables:
@@ -238,13 +231,14 @@
         return carry
 
     lax.fori_loop(0, TILES, fetch, 0)
-    heights = height_ref[...]
+    heights = jnp.sum(height_ref[...], axis=0)
     mean = jnp.sum(heights, keepdims=True) * (1.0 / (SC * SC))
     height_row = lax.broadcasted_iota(jnp.int32, heights.shape, 0)
     height_lane = lax.broadcasted_iota(jnp.int32, heights.shape, 1)
 
     for table in tables:
         table.wait()
+    left_ref[...] = right_ref[...].T
     for at in range(4):
         rows = slice(at * NF, (at + 1) * NF)
         block = right_ref[(at // 2) * NF : (at // 2 + 1) * NF]
@@ -298,7 +292,7 @@
 def image(place, labels, centre, heights, spectra, pieces):
     return pl.pallas_call(
         image_kernel,
-        in_specs=[SMEM] * 6 + [VMEM, ANY, HBM, HBM] + [ANY] * 8,
+        in_specs=[SMEM] * 6 + [VMEM, ANY, HBM] + [ANY] * 8,
         out_specs=VMEM,
         out_shape=jax.ShapeDtypeStruct((TILES, Q, Q), BF16),
         scratch_shapes=[
@@ -308,12 +302,12 @@
             pltpu.VMEM((2 * NF, 2 * Q), BF16),
             pltpu.VMEM((4 * NF, 4 * Q), BF16),
             pltpu.SemaphoreType.DMA((TILES,)),
-            pltpu.SemaphoreType.DMA((3,)),
+            pltpu.SemaphoreType.DMA((2,)),
         ],
         name="image",
         compiler_params=pltpu.CompilerParams(vmem_limit_bytes=16 << 20),
         cost_estimate=pl.CostEstimate(flops=3 * 10**9, bytes_accessed=4 * 10**6, transcendentals=0),
-    )(*place, labels, centre, heights, spectra, as_bf16(left_table()), as_bf16(image_table()), *pieces)
+    )(*place, labels, centre, heights, spectra, as_bf16(image_table()), *pieces)
 
 
 def resist_kernel(
@@ -406,10 +400,8 @@
     return lax.ppermute(x, "tile", [(t, t ^ 1) for t in range(8)])
 
 
-def summed(x, axis):
-    size = lax.axis_size(axis)
-    copies = jnp.broadcast_to(x[None], (size, *x.shape))
-    return jnp.sum(lax.all_to_all(copies, axis, 0, 0, tiled=True), axis=0)
+def exchange(copies, axis):
+    return lax.all_to_all(copies, axis, 0, 0, tiled=True)
 
 
 def device_steps(mask_tiles, class_of_tile, cell_of_tile, kernels, class_center):
@@ -433,18 +425,19 @@
     before = send(mine, 0, 1)
     after = send(mine, 0, -1)
     far = send(mine, 0, 2)
-    heights = density_heights(mask_tiles, cell_of_tile)
+    heights = density_heights(mask_tiles, cell_of_tile, lax.axis_size("tile"))
     low = jnp.stack([mine, after_all(before, heights)])
     high = jnp.stack([after_all(far, heights), after])
     low_before = send(low, 1, 1)
     high_after = send(high, 1, -1)
     high_before = send(high, 1, 1)
     low_after = send(low, 1, -1)
-    heights = summed(heights, "tile")
+    low_far = send(low_before, 1, 1)
+    high_far = send(high_after, 1, -1)
+    heights = jnp.sum(exchange(heights, "tile"), axis=0)
+    heights = jnp.broadcast_to(heights[None], (lax.axis_size("focus"), *heights.shape))
+    heights = exchange(heights, "focus")
     spectra = form_spectra(mask_tiles)
-    low_far = send(after_all(low_before, heights), 1, 1)
-    high_far = send(after_all(high_after, heights), 1, -1)
-    heights = summed(heights, "focus")
     other_spectra = partner(spectra)
     pieces = (low, high, low_before, high_before, low_far, high_far, low_after, high_after)
     other = image(place, other_labels, class_center, heights, other_spectra, pieces)

time: 77.2 us -> 80.9 us (1.048)
  waiting for transfers between devices: 9.06 us -> 16.4 us
  blocking collectives: 11.7 us -> 10.4 us
  other arithmetic: 2.13 us -> 1.28 us
    ppermute x9, waiting for transfers between devices: 2.03 us -> 9.92 us  [send(): return lax.ppermute(value, ALL, ring(phase, step))]
    all_to_all x1, blocking collectives: 11.7 us -> 10.4 us  [exchange(): return lax.all_to_all(copies, axis, 0, 0, tiled=True)]
    all_to_all x1, starting transfers between devices: 4.55 us -> 3.59 us  [exchange(): return lax.all_to_all(copies, axis, 0, 0, tiled=True)]
    reduce_sum x2 -> x1, other arithmetic: 0.87 us -> 0.01 us  [device_steps(): heights = jnp.sum(exchange(heights, 'tile'), axis=0)]
  transfers between devices with their start and end apart: 13 -> 13, of which waited for: 2 -> 4; matrix products, arithmetic and copies ran while one was open for 5% -> 3% of each run, Pallas kernels for 20% -> 19%
where the time goes in v3:
time: 80.9 us; the launch traced here: 80.6 us
  Pallas kernels  25.3 us (31%)
  starting transfers between devices  22.8 us (28%)
  waiting for transfers between devices  16.4 us (20%)
  blocking collectives  10.4 us (13%)
  local copies, waits for them, and re-layouts  4.14 us (5%)
  other arithmetic  1.28 us (2%)
    ppermute x9, starting transfers between devices, send(): return lax.ppermute(value, ALL, ring(phase, step))  14.1 us
    pallas_call x2, Pallas kernels, image(): pl.pallas_call(image_kernel, in_specs=[SMEM] * 6 + [VMEM, ANY, HBM] + [AN...  12 us
    all_to_all x1, blocking collectives, exchange(): return lax.all_to_all(copies, axis, 0, 0, tiled=True)  10.4 us
    ppermute x9, waiting for transfers between devices, send(): return lax.ppermute(value, ALL, ring(phase, step))  9.92 us
    all_to_all x1, waiting for transfers between devices, exchange(): return lax.all_to_all(copies, axis, 0, 0, tiled=True)  6.51 us
    pallas_call x1, Pallas kernels, form_spectra(): pl.pallas_call(functools.partial(spectra_kernel, step), in_specs=[HBM] *...  5.15 us
    ppermute x3, starting transfers between devices, partner(): return lax.ppermute(x, 'tile', [(t, t ^ 1) for t in range(8)])  5.1 us
    pallas_call x1, Pallas kernels, density_heights(): pl.pallas_call(density_kernel, in_specs=[SMEM] + [HBM] * 3, out_specs=VME...  4.45 us
  transfers between devices with their start and end apart: 13, of which 4 were waited for; matrix products, arithmetic and copies ran while one was open for 3% of the time, Pallas kernels for 19%

profile of v3, /device:TPU:1, one launch (start us, length us, event | category | flops | bytes accessed | tf_op | source)
XLA Modules:
  0.0 80.6 jit_solution(15919798174868394886)
XLA Ops:
  0.0 1.1 %copy-done = bf16[1,24,4,4096]{3,2,1,0:T(4,128)(2,1)S(1)} copy-done((bf16[1,24,4,4096]{3,2,1,0:T(4,128)(2,1)S(1)}, bf16[1,24,4,4096]{3,2,1,0:T(4,128)(2,1)}, u32[]{:S(2)}) %copy-start) | copy-done | bytes 786456
  1.1 0.2 constant_dynamic-slice_fusion
  1.3 0.6 reshape.27
  1.9 0.6 copy.14
  2.5 0.5 reshape.28
  3.0 0.0 copy-start.8
  3.0 0.0 copy-start.9
  3.0 3.6 %collective-permute-start.1 = (bf16[3,4,64,256]{3,2,1,0:T(8,128)(2,1)S(1)}, bf16[3,4,64,256]{3,2,1,0:T(8,128)(2,1)S(1)}, u32[]{:S(2)}, u32[]{:S(2)}) collective-permute-start(bf16[3,4,64,256]{3,2,1,0:T(8,128)(2,1)S(1)} %reshape.28), channel_id=1, source_target_pairs={{0,2},{1,3},{2,0},{3,1},{4,6},{5,7},{6,4},{7,5},{8,10},{9,11},{10,... | collective-permute-start | bytes 1179656 | tf_op jit(solution)/shard_map/ppermute | solution.py:392
  6.7 0.3 collective-permute-start
  7.0 2.4 %collective-permute-start.2 = (bf16[3,4,64,256]{3,2,1,0:T(8,128)(2,1)S(1)}, bf16[3,4,64,256]{3,2,1,0:T(8,128)(2,1)}, u32[]{:S(2)}, u32[]{:S(2)}) collective-permute-start(bf16[3,4,64,256]{3,2,1,0:T(8,128)(2,1)S(1)} %reshape.28), channel_id=1, source_target_pairs={{0,3},{1,0},{2,1},{3,2},{4,7},{5,4},{6,5},{7,6},{8,11},{9,8},{10,9... | collective-permute-start | bytes 1179656 | tf_op jit(solution)/shard_map/ppermute | solution.py:392
  9.4 0.5 stack_reshape.3
  9.8 4.5 %density.1 = f32[8,8,128]{2,1,0:T(8,128)} custom-call(s32[8]{0:T(128)} %cell_ref.1, bf16[8,512,512]{2,1,0:T(8,128)(2,1)} %mask_hbm.3, f32[32,8,128]{2,1,0:T(8,128)} %constant.68.clone.row_hbm, f32[32,8,128]{2,1,0:T(8,128)} %constant.69.clone.col_hbm), custom_call_target="tpu_custom_call" | custom-call | flops 10000000 | bytes 5000000 | tf_op jit(solution)/shard_map/density/pallas_call | solution.py:131
  14.3 0.0 copy-start.4
  14.3 0.0 copy-start.5
  14.3 0.0 collective-permute-done.1
  14.3 0.0 copy-start.6
  14.4 2.0 %collective-permute-done = bf16[3,4,64,256]{3,2,1,0:T(8,128)(2,1)S(1)} collective-permute-done((bf16[3,4,64,256]{3,2,1,0:T(8,128)(2,1)S(1)}, bf16[3,4,64,256]{3,2,1,0:T(8,128)(2,1)S(1)}, u32[]{:S(2)}, u32[]{:S(2)}) %collective-permute-start) | collective-permute-done | bytes 393248 | tf_op jit(solution)/shard_map/ppermute | solution.py:392
  16.4 0.1 pad_maximum_fusion.rest_0_
  16.4 1.3 %collective-permute-start.3 = (bf16[2,3,4,64,256]{4,3,2,1,0:T(8,128)(2,1)S(1)}, bf16[2,3,4,64,256]{4,3,2,1,0:T(8,128)(2,1)S(1)}, u32[]{:S(2)}, u32[]{:S(2)}) collective-permute-start(bf16[2,3,4,64,256]{4,3,2,1,0:T(8,128)(2,1)S(1)} %pad_maximum_fusion.rest_0_), channel_id=1, source_target_pairs={{0,4},{1,5},{2,6},{3,7},{4,8},{5,9},{6,10},{7,11},{8,12},{9,13},{1... | collective-permute-start | bytes 2359304 | tf_op jit(solution)/shard_map/ppermute | solution.py:392
  17.7 0.0 collective-permute-done.2
  17.7 1.2 %pad_maximum_fusion.1.rest_1_ = bf16[2,3,4,64,256]{4,3,2,1,0:T(8,128)(2,1)S(1)} fusion(bf16[1,3,4,64,256]{4,3,2,1,0:T(8,128)(2,1)} %bitcast.8, bf16[1,3,4,64,256]{4,3,2,1,0:T(8,128)(2,1)} %bitcast.11), kind=kLoop, calls=%fused_computation.1 | loop fusion | flops 393216 | bytes 1572864 | tf_op jit(solution)/shard_map/stack | solution.py:430
  18.9 1.9 %collective-permute-start.6 = (bf16[2,3,4,64,256]{4,3,2,1,0:T(8,128)(2,1)S(1)}, bf16[2,3,4,64,256]{4,3,2,1,0:T(8,128)(2,1)}, u32[]{:S(2)}, u32[]{:S(2)}) collective-permute-start(bf16[2,3,4,64,256]{4,3,2,1,0:T(8,128)(2,1)S(1)} %pad_maximum_fusion.1.rest_1_), channel_id=1, source_target_pairs={{0,12},{1,13},{2,14},{3,15},{4,0},{5,1},{6,2},{7,3},{8,4},{9,5},{1... | collective-permute-start | bytes 2359304 | tf_op jit(solution)/shard_map/ppermute | solution.py:392
  20.9 1.4 %collective-permute-start.8 = (bf16[2,3,4,64,256]{4,3,2,1,0:T(8,128)(2,1)S(1)}, bf16[2,3,4,64,256]{4,3,2,1,0:T(8,128)(2,1)}, u32[]{:S(2)}, u32[]{:S(2)}) collective-permute-start(bf16[2,3,4,64,256]{4,3,2,1,0:T(8,128)(2,1)S(1)} %pad_maximum_fusion.rest_0_), channel_id=1, source_target_pairs={{0,12},{1,13},{2,14},{3,15},{4,0},{5,1},{6,2},{7,3},{8,4},{9,5},{1... | collective-permute-start | bytes 2359304 | tf_op jit(solution)/shard_map/ppermute | solution.py:392
  22.3 0.0 collective-permute-start.4
  22.3 6.9 %collective-permute-done.3.rest_2_ = bf16[2,3,4,64,256]{4,3,2,1,0:T(8,128)(2,1)S(1)} collective-permute-done((bf16[2,3,4,64,256]{4,3,2,1,0:T(8,128)(2,1)S(1)}, bf16[2,3,4,64,256]{4,3,2,1,0:T(8,128)(2,1)S(1)}, u32[]{:S(2)}, u32[]{:S(2)}) %collective-permute-start.3) | collective-permute-done | bytes 786464 | tf_op jit(solution)/shard_map/ppermute | solution.py:392
  29.2 0.0 collective-permute-start.5
  29.2 1.0 %collective-permute-done.6.rest_7_ = bf16[2,3,4,64,256]{4,3,2,1,0:T(8,128)(2,1)} collective-permute-done((bf16[2,3,4,64,256]{4,3,2,1,0:T(8,128)(2,1)S(1)}, bf16[2,3,4,64,256]{4,3,2,1,0:T(8,128)(2,1)}, u32[]{:S(2)}, u32[]{:S(2)}) %collective-permute-start.6) | collective-permute-done | bytes 786464 | tf_op jit(solution)/shard_map/ppermute | solution.py:392
  30.2 3.1 %collective-permute-start.7 = (bf16[2,3,4,64,256]{4,3,2,1,0:T(8,128)(2,1)}, bf16[2,3,4,64,256]{4,3,2,1,0:T(8,128)(2,1)}, u32[]{:S(2)}, u32[]{:S(2)}) collective-permute-start(bf16[2,3,4,64,256]{4,3,2,1,0:T(8,128)(2,1)} %collective-permute-done.6.rest_7_), channel_id=1, source_target_pairs={{0,12},{1,13},{2,14},{3,15},{4,0},{5,1},{6,2},{7,3},{8,4},{9,5},{1... | collective-permute-start | bytes 2359304 | tf_op jit(solution)/shard_map/ppermute | solution.py:392
  33.3 2.7 %collective-permute-start.9 = (s32[8]{0:T(128)S(1)}, s32[8]{0:T(128)S(1)}, u32[]{:S(2)}, u32[]{:S(2)}) collective-permute-start(s32[8]{0:T(128)S(1)} %bitcast_add_fusion.label_ref), channel_id=1, source_target_pairs={{0,16},{16,0},{32,48},{48,32},{64,80},{80,64},{96,112},{112,96},{1... | collective-permute-start | bytes 104 | tf_op jit(solution)/shard_map/ppermute | solution.py:400
  36.0 5.1 %spectra.1.spec_hbm = bf16[8,2,64,128]{3,2,1,0:T(8,128)(2,1)} custom-call(bf16[8,512,512]{2,1,0:T(8,128)(2,1)} %mask_hbm.3, bf16[512,128]{1,0:T(8,128)(2,1)} %constant.79.wave_t_hbm, bf16[128,512]{1,0:T(8,128)(2,1)} %constant.80.wave_hbm), custom_call_target="tpu_custom_call" | custom-call | flops 1000000000 | bytes 5000000 | tf_op jit(solution)/shard_map/spectra/pallas_call | solution.py:189
  41.2 0.0 collective-permute-done.9.label_ref
  41.2 0.1 collective-permute-start.10
  41.3 10.4 %all_to_all.10 = f32[8,8,128]{2,1,0:T(8,128)S(1)} all-to-all(f32[8,8,128]{2,1,0:T(8,128)S(1)} %copy-done.7), channel_id=1, replica_groups=mesh['tile'=8,'focus'=16] {'tile'}, dimensions={0} | all-to-all | bytes 65536 | tf_op jit(solution)/shard_map/all_to_all | solution.py:404
  51.7 0.6 broadcast_in_dim.2
  52.4 3.6 %all-to-all-start.1 = ((f32[16,8,128]{2,1,0:T(8,128)}), f32[16,8,128]{2,1,0:T(8,128)S(1)}, u32[]{:S(2)}, u32[]{:S(2)}) async-start(f32[16,8,128]{2,1,0:T(8,128)} %broadcast_in_dim.2), calls=%async_computation.1 | async-start | bytes 131072 | tf_op jit(solution)/shard_map/all_to_all | solution.py:404
  56.0 6.5 %all-to-all-done.1.height_ref = f32[16,8,128]{2,1,0:T(8,128)S(1)} async-done(((f32[16,8,128]{2,1,0:T(8,128)}), f32[16,8,128]{2,1,0:T(8,128)S(1)}, u32[]{:S(2)}, u32[]{:S(2)}) %all-to-all-start.1) | async-done | bytes 65568 | tf_op jit(solution)/shard_map/all_to_all | solution.py:404
  62.5 0.0 collective-permute-done.10.spec_hbm
  62.5 0.0 collective-permute-done.8.rest_6_
  62.5 0.0 collective-permute-done.4.rest_3_
  62.5 0.0 collective-permute-done.5.rest_4_
  62.5 0.0 collective-permute-done.7.rest_5_
  62.6 0.0 copy-start.1
  62.6 6.0 %image.3 = bf16[8,128,128]{2,1,0:T(8,128)(2,1)S(1)} custom-call(s32[1]{0:T(128)} %bitcast.first_ref, s32[1]{0:T(128)} %bitcast.1.second_ref, s32[1]{0:T(128)} %bitcast.2.first_div_ref, s32[1]{0:T(128)} %bitcast.3.second_div_ref, s32[8]{0:T(128)S(1)} %collective-permute-done.9.label_ref, f32[16]{0:T(128)S(1)} %copy-done.4, ...), custom_call_target="tpu_custom_call" | custom-call | flops 3000000000 | bytes 4000000 | tf_op jit(solution)/shard_map/image/pallas_call | solution.py:293
  68.5 0.0 copy-start.2
  68.6 0.0 copy-start.3
  68.6 2.3 %collective-permute-start.11 = (bf16[8,128,128]{2,1,0:T(8,128)(2,1)S(1)}, bf16[8,128,128]{2,1,0:T(8,128)(2,1)S(1)}, u32[]{:S(2)}, u32[]{:S(2)}) collective-permute-start(bf16[8,128,128]{2,1,0:T(8,128)(2,1)S(1)} %image.3), channel_id=1, source_target_pairs={{0,16},{16,0},{32,48},{48,32},{64,80},{80,64},{96,112},{112,96},{1... | collective-permute-start | bytes 786440 | tf_op jit(solution)/shard_map/ppermute | solution.py:400
  70.9 6.1 %image.2.own_hbm = bf16[8,128,128]{2,1,0:T(8,128)(2,1)S(1)} custom-call(s32[1]{0:T(128)} %bitcast.first_ref, s32[1]{0:T(128)} %bitcast.1.second_ref, s32[1]{0:T(128)} %bitcast.2.first_div_ref, s32[1]{0:T(128)} %bitcast.3.second_div_ref, s32[8]{0:T(128)S(1)} %bitcast_add_fusion.label_ref, f32[16]{0:T(128)S(1)} %copy-done.4, ...), custom_call_target="tpu_custom_call" | custom-call | flops 3000000000 | bytes 4000000 | tf_op jit(solution)/shard_map/image/pallas_call | solution.py:293
  77.0 3.6 %resist.1 = bf16[8,512,512]{2,1,0:T(8,128)(2,1)} custom-call(bf16[8,128,128]{2,1,0:T(8,128)(2,1)S(1)} %image.2.own_hbm, bf16[8,128,128]{2,1,0:T(8,128)(2,1)S(1)} %collective-permute-done.11.other_hbm, bf16[512,128]{1,0:T(8,128)(2,1)S(1)} %copy-done.3, bf16[128,512]{1,0:T(8,128)(2,1)S(1)} %copy-done.2), custom_call_target="tpu_custom_call" | custom-call | flops 1000000000 | bytes 5000000 | tf_op jit(solution)/shard_map/resist/pallas_call | solution.py:355
  (14 shorter events, 0.0 us)
Async XLA Ops:
  0.0 1.1 %copy-start = (bf16[1,24,4,4096]{3,2,1,0:T(4,128)(2,1)S(1)}, bf16[1,24,4,4096]{3,2,1,0:T(4,128)(2,1)}, u32[]{:S(2)}) copy-start(bf16[1,24,4,4096]{3,2,1,0:T(4,128)(2,1)} %param.16) | copy-start | bytes 2359300
  3.0 30.3 %copy-start.8 = (s32[8]{0:T(128)S(1)}, s32[8]{0:T(128)}, u32[]{:S(2)}) copy-start(s32[8]{0:T(128)} %cell_ref.1) | copy-start | bytes 100
  3.0 30.3 %copy-start.9 = (s32[8,1]{0,1:T(1,128)S(1)}, s32[8,1]{0,1:T(1,128)}, u32[]{:S(2)}) copy-start(s32[8,1]{0,1:T(1,128)} %param.14) | copy-start | bytes 100
  3.0 11.3 %collective-permute-start.1 = (bf16[3,4,64,256]{3,2,1,0:T(8,128)(2,1)S(1)}, bf16[3,4,64,256]{3,2,1,0:T(8,128)(2,1)S(1)}, u32[]{:S(2)}, u32[]{:S(2)}) collective-permute-start(bf16[3,4,64,256]{3,2,1,0:T(8,128)(2,1)S(1)} %reshape.28), channel_id=1, source_target_pairs={{0,2},{1,3},{2,0},{3,1},{4,6},{5,7},{6,4},{7,5},{8,10},{9,11},{10,... | collective-permute-start | bytes 1179656 | tf_op jit(solution)/shard_map/ppermute | solution.py:392
  6.7 9.7 %collective-permute-start = (bf16[3,4,64,256]{3,2,1,0:T(8,128)(2,1)S(1)}, bf16[3,4,64,256]{3,2,1,0:T(8,128)(2,1)S(1)}, u32[]{:S(2)}, u32[]{:S(2)}) collective-permute-start(bf16[3,4,64,256]{3,2,1,0:T(8,128)(2,1)S(1)} %reshape.28), channel_id=1, source_target_pairs={{0,1},{1,2},{2,3},{3,0},{4,5},{5,6},{6,7},{7,4},{8,9},{9,10},{10,1... | collective-permute-start | bytes 1179656 | tf_op jit(solution)/shard_map/ppermute | solution.py:392
  7.0 10.7 %collective-permute-start.2 = (bf16[3,4,64,256]{3,2,1,0:T(8,128)(2,1)S(1)}, bf16[3,4,64,256]{3,2,1,0:T(8,128)(2,1)}, u32[]{:S(2)}, u32[]{:S(2)}) collective-permute-start(bf16[3,4,64,256]{3,2,1,0:T(8,128)(2,1)S(1)} %reshape.28), channel_id=1, source_target_pairs={{0,3},{1,0},{2,1},{3,2},{4,7},{5,4},{6,5},{7,6},{8,11},{9,8},{10,9... | collective-permute-start | bytes 1179656 | tf_op jit(solution)/shard_map/ppermute | solution.py:392
  14.3 27.0 %copy-start.7 = (f32[8,8,128]{2,1,0:T(8,128)S(1)}, f32[8,8,128]{2,1,0:T(8,128)}, u32[]{:S(2)}) copy-start(f32[8,8,128]{2,1,0:T(8,128)} %density.1) | copy-start | bytes 98308
  14.3 48.2 %copy-start.4 = (f32[16]{0:T(128)S(1)}, f32[16]{0:T(128)}, u32[]{:S(2)}) copy-start(f32[16]{0:T(128)} %centre_ref.3) | copy-start | bytes 196
  14.3 48.2 %copy-start.5 = (bf16[128,256]{1,0:T(8,128)(2,1)S(1)}, bf16[128,256]{1,0:T(8,128)(2,1)}, u32[]{:S(2)}) copy-start(bf16[128,256]{1,0:T(8,128)(2,1)} %constant.81.right_hbm) | copy-start | bytes 196612
  14.3 3.4 %copy-start.6 = (bf16[3,4,64,256]{3,2,1,0:T(8,128)(2,1)}, bf16[3,4,64,256]{3,2,1,0:T(8,128)(2,1)S(1)}, u32[]{:S(2)}) copy-start(bf16[3,4,64,256]{3,2,1,0:T(8,128)(2,1)S(1)} %collective-permute-done.1) | copy-start | bytes 1179652
  16.4 12.8 %collective-permute-start.3 = (bf16[2,3,4,64,256]{4,3,2,1,0:T(8,128)(2,1)S(1)}, bf16[2,3,4,64,256]{4,3,2,1,0:T(8,128)(2,1)S(1)}, u32[]{:S(2)}, u32[]{:S(2)}) collective-permute-start(bf16[2,3,4,64,256]{4,3,2,1,0:T(8,128)(2,1)S(1)} %pad_maximum_fusion.rest_0_), channel_id=1, source_target_pairs={{0,4},{1,5},{2,6},{3,7},{4,8},{5,9},{6,10},{7,11},{8,12},{9,13},{1... | collective-permute-start | bytes 2359304 | tf_op jit(solution)/shard_map/ppermute | solution.py:392
  18.9 11.3 %collective-permute-start.6 = (bf16[2,3,4,64,256]{4,3,2,1,0:T(8,128)(2,1)S(1)}, bf16[2,3,4,64,256]{4,3,2,1,0:T(8,128)(2,1)}, u32[]{:S(2)}, u32[]{:S(2)}) collective-permute-start(bf16[2,3,4,64,256]{4,3,2,1,0:T(8,128)(2,1)S(1)} %pad_maximum_fusion.1.rest_1_), channel_id=1, source_target_pairs={{0,12},{1,13},{2,14},{3,15},{4,0},{5,1},{6,2},{7,3},{8,4},{9,5},{1... | collective-permute-start | bytes 2359304 | tf_op jit(solution)/shard_map/ppermute | solution.py:392
  20.9 41.7 %collective-permute-start.8 = (bf16[2,3,4,64,256]{4,3,2,1,0:T(8,128)(2,1)S(1)}, bf16[2,3,4,64,256]{4,3,2,1,0:T(8,128)(2,1)}, u32[]{:S(2)}, u32[]{:S(2)}) collective-permute-start(bf16[2,3,4,64,256]{4,3,2,1,0:T(8,128)(2,1)S(1)} %pad_maximum_fusion.rest_0_), channel_id=1, source_target_pairs={{0,12},{1,13},{2,14},{3,15},{4,0},{5,1},{6,2},{7,3},{8,4},{9,5},{1... | collective-permute-start | bytes 2359304 | tf_op jit(solution)/shard_map/ppermute | solution.py:392
  22.3 40.2 %collective-permute-start.4 = (bf16[2,3,4,64,256]{4,3,2,1,0:T(8,128)(2,1)S(1)}, bf16[2,3,4,64,256]{4,3,2,1,0:T(8,128)(2,1)}, u32[]{:S(2)}, u32[]{:S(2)}) collective-permute-start(bf16[2,3,4,64,256]{4,3,2,1,0:T(8,128)(2,1)S(1)} %pad_maximum_fusion.1.rest_1_), channel_id=1, source_target_pairs={{0,4},{1,5},{2,6},{3,7},{4,8},{5,9},{6,10},{7,11},{8,12},{9,13},{1... | collective-permute-start | bytes 2359304 | tf_op jit(solution)/shard_map/ppermute | solution.py:392
  29.2 33.3 %collective-permute-start.5 = (bf16[2,3,4,64,256]{4,3,2,1,0:T(8,128)(2,1)S(1)}, bf16[2,3,4,64,256]{4,3,2,1,0:T(8,128)(2,1)}, u32[]{:S(2)}, u32[]{:S(2)}) collective-permute-start(bf16[2,3,4,64,256]{4,3,2,1,0:T(8,128)(2,1)S(1)} %collective-permute-done.3.rest_2_), channel_id=1, source_target_pairs={{0,4},{1,5},{2,6},{3,7},{4,8},{5,9},{6,10},{7,11},{8,12},{9,13},{1... | collective-permute-start | bytes 2359304 | tf_op jit(solution)/shard_map/ppermute | solution.py:392
  30.2 32.3 %collective-permute-start.7 = (bf16[2,3,4,64,256]{4,3,2,1,0:T(8,128)(2,1)}, bf16[2,3,4,64,256]{4,3,2,1,0:T(8,128)(2,1)}, u32[]{:S(2)}, u32[]{:S(2)}) collective-permute-start(bf16[2,3,4,64,256]{4,3,2,1,0:T(8,128)(2,1)} %collective-permute-done.6.rest_7_), channel_id=1, source_target_pairs={{0,12},{1,13},{2,14},{3,15},{4,0},{5,1},{6,2},{7,3},{8,4},{9,5},{1... | collective-permute-start | bytes 2359304 | tf_op jit(solution)/shard_map/ppermute | solution.py:392
  33.3 7.9 %collective-permute-start.9 = (s32[8]{0:T(128)S(1)}, s32[8]{0:T(128)S(1)}, u32[]{:S(2)}, u32[]{:S(2)}) collective-permute-start(s32[8]{0:T(128)S(1)} %bitcast_add_fusion.label_ref), channel_id=1, source_target_pairs={{0,16},{16,0},{32,48},{48,32},{64,80},{80,64},{96,112},{112,96},{1... | collective-permute-start | bytes 104 | tf_op jit(solution)/shard_map/ppermute | solution.py:400
  41.2 21.3 %collective-permute-start.10 = (bf16[8,2,64,128]{3,2,1,0:T(8,128)(2,1)}, bf16[8,2,64,128]{3,2,1,0:T(8,128)(2,1)S(1)}, u32[]{:S(2)}, u32[]{:S(2)}) collective-permute-start(bf16[8,2,64,128]{3,2,1,0:T(8,128)(2,1)} %spectra.1.spec_hbm), channel_id=1, source_target_pairs={{0,16},{16,0},{32,48},{48,32},{64,80},{80,64},{96,112},{112,96},{1... | collective-permute-start | bytes 786440 | tf_op jit(solution)/shard_map/ppermute | solution.py:400
  52.4 10.1 %all-to-all-start.1 = ((f32[16,8,128]{2,1,0:T(8,128)}), f32[16,8,128]{2,1,0:T(8,128)S(1)}, u32[]{:S(2)}, u32[]{:S(2)}) async-start(f32[16,8,128]{2,1,0:T(8,128)} %broadcast_in_dim.2), calls=%async_computation.1 | async-start | bytes 131072 | tf_op jit(solution)/shard_map/all_to_all | solution.py:404
  62.6 8.3 %copy-start.1 = (bf16[8,2,64,128]{3,2,1,0:T(8,128)(2,1)S(1)}, bf16[8,2,64,128]{3,2,1,0:T(8,128)(2,1)}, u32[]{:S(2)}) copy-start(bf16[8,2,64,128]{3,2,1,0:T(8,128)(2,1)} %spectra.1.spec_hbm) | copy-start | bytes 786436
  68.5 8.4 %copy-start.2 = (bf16[128,512]{1,0:T(8,128)(2,1)S(1)}, bf16[128,512]{1,0:T(8,128)(2,1)}, u32[]{:S(2)}) copy-start(bf16[128,512]{1,0:T(8,128)(2,1)} %constant.83.resist_t_hbm) | copy-start | bytes 393220
  68.6 8.4 %copy-start.3 = (bf16[512,128]{1,0:T(8,128)(2,1)S(1)}, bf16[512,128]{1,0:T(8,128)(2,1)}, u32[]{:S(2)}) copy-start(bf16[512,128]{1,0:T(8,128)(2,1)} %constant.82.resist_hbm) | copy-start | bytes 393220
  68.6 8.4 %collective-permute-start.11 = (bf16[8,128,128]{2,1,0:T(8,128)(2,1)S(1)}, bf16[8,128,128]{2,1,0:T(8,128)(2,1)S(1)}, u32[]{:S(2)}, u32[]{:S(2)}) collective-permute-start(bf16[8,128,128]{2,1,0:T(8,128)(2,1)S(1)} %image.3), channel_id=1, source_target_pairs={{0,16},{16,0},{32,48},{48,32},{64,80},{80,64},{96,112},{112,96},{1... | collective-permute-start | bytes 786440 | tf_op jit(solution)/shard_map/ppermute | solution.py:400
